TPU v7x, 768 devices: a whole 4x8x12 slice. The times are simulated.
768 devices in a mesh: dom: 12 (over z), grp: 64 (over y, x, core).
Axes of the slice: x: 4, y: 8, z: 12, core: 2. Of those that a mesh axis runs over, the one named last changes fastest.
Arguments:
- support: float32 [16, 16, 16, 98304], P(None, None, None, ('dom', 'grp')), may hold values from -6 to 6
- potential: float32 [16, 16, 16, 98304], P(None, None, None, ('dom', 'grp')), may hold values from -6 to 6
- magic_taps: float32 [16], replicated, may hold values from -1 to 1
- kinetic_taps: float32 [16], replicated, may hold values from -1 to 1
- kernel_diag: float32 [98304], P(('dom', 'grp')), may hold values from 0.2 to 5
- owners: int32 [98304, 1], P(('dom', 'grp')), may hold values from 0 to 63; in each aligned block of 128 rows (0 to 127, 128 to 255, ...) at most 3 rows name the same one
Outputs:
- margin: float32 [98304, 128], P(('dom', 'grp'))
- density: float32 [96, 256], P('dom')
Inputs may be any that keep to these rules, and one draw needn't show every extreme that they name: `owners`: within each device's aligned block of 128 functions, no owner is named by more than 3 functions, a bound that some block reaches.
All inputs are finite; a program needn't handle non-finite values.
Results may differ from a plain program's by a relative error of at most 0.004.
Values may be sent and summed in bfloat16 or wider, within the bound.
No kernel may reach another device: no remote copies, remote signals or barrier semaphores. Data moves between devices by JAX's collectives and lax.ppermute only.
A program may use at most 32 MiB of HBM per device.

v0:
```python
import jax
import jax.numpy as jnp
from jax import lax
from jax.sharding import PartitionSpec as P

HIGHEST = lax.Precision.HIGHEST


def passed_along(block, axis, distance):
    devices = range(lax.axis_size(axis))
    route = [((i - distance) % len(devices), i) for i in devices]
    return lax.ppermute(block, axis, route)


def band_matrix(tap_values, box_side):
    row_index = jnp.arange(box_side)[:, None]
    col_index = jnp.arange(box_side)[None, :]
    offset = col_index - row_index + (tap_values.shape[0] // 2 - 1)
    tap_table = (offset[:, :, None] == jnp.arange(tap_values.shape[0])[None, None, :]).astype(
        jnp.float32
    )
    return jnp.einsum("abt,t->ab", tap_table, tap_values, precision=HIGHEST)


def filter_along(matrix, field_block, direction):
    if direction == 0:
        return jnp.einsum("ab,bjkf->ajkf", matrix, field_block, precision=HIGHEST)
    if direction == 1:
        return jnp.einsum("ab,ibkf->iakf", matrix, field_block, precision=HIGHEST)
    return jnp.einsum("ab,ijbf->ijaf", matrix, field_block, precision=HIGHEST)


def apply_block(support, potential, magic_taps, kinetic_taps, kernel_diag):
    box_side = support.shape[0]
    magic_band = band_matrix(magic_taps, box_side)
    kinetic_band = band_matrix(kinetic_taps, box_side)
    realspace = filter_along(
        magic_band, filter_along(magic_band, filter_along(magic_band, support, 0), 1), 2
    )
    density_part = jnp.sum(kernel_diag * realspace * realspace, axis=3)
    weighted = potential * realspace
    magic_back = magic_band.T
    returned = filter_along(
        magic_back, filter_along(magic_back, filter_along(magic_back, weighted, 0), 1), 2
    )
    kinetic_part = (
        filter_along(kinetic_band, support, 0)
        + filter_along(kinetic_band, support, 1)
        + filter_along(kinetic_band, support, 2)
    )
    gradient = (returned + kinetic_part).astype(jnp.bfloat16)
    return (gradient, density_part)


def body(support, potential, magic_taps, kinetic_taps, kernel_diag, owners):
    box_side = support.shape[0]
    local_count = support.shape[3]
    cell_count = box_side**3
    half_side = box_side // 2
    groups = lax.axis_size("grp")
    capacity = max(2, 3 * local_count // (2 * groups))
    scale_factor = 1.0 / float(box_side) ** 1.5
    gradient, density_part = apply_block(support, potential, magic_taps, kinetic_taps, kernel_diag)
    density_part = (density_part / (local_count * groups)).reshape(box_side, box_side * box_side)
    target = owners[:, 0]
    onehot = (target[:, None] == jnp.arange(groups)[None, :]).astype(jnp.int32)
    before = jnp.cumsum(onehot, axis=0) - onehot
    slot_index = jnp.sum(before * onehot, axis=1)
    column = target * capacity + slot_index
    dispatch = (column[:, None] == jnp.arange(groups * capacity)[None, :]).astype(jnp.bfloat16)
    gradient_flat = gradient.reshape(cell_count, local_count)
    outgoing = lax.dot_general(
        dispatch, gradient_flat, (((0,), (1,)), ((), ())), preferred_element_type=jnp.float32
    ).astype(jnp.bfloat16)
    owned = support.reshape(cell_count, local_count).astype(jnp.bfloat16)
    received = lax.all_to_all(outgoing, "grp", split_axis=0, concat_axis=0, tiled=True)
    products = jnp.dot(received, owned, preferred_element_type=jnp.float32)
    products = products * (kernel_diag * scale_factor)[None, :]
    returned_rows = lax.all_to_all(products, "grp", split_axis=0, concat_axis=0, tiled=True)
    margin = jnp.dot(dispatch.astype(jnp.float32), returned_rows, precision=HIGHEST)
    summed = lax.psum(density_part, "grp")
    density_slab = summed[:half_side] + passed_along(summed[half_side:], "dom", 1)
    return (margin, density_slab)


def solution(mesh):
    return jax.shard_map(
        body,
        mesh=mesh,
        in_specs=(
            P(None, None, None, ("dom", "grp")),
            P(None, None, None, ("dom", "grp")),
            P(),
            P(),
            P(("dom", "grp")),
            P(("dom", "grp"), None),
        ),
        out_specs=(P(("dom", "grp"), None), P("dom", None)),
        check_vma=False,
    )
```

profile of v0, /device:TPU:1, one launch (start us, length us, event | category | flops | bytes accessed | tf_op | source)
XLA Modules:
  0.0 374.1 jit_solution(15786044467806329147)
XLA Ops:
  0.6 0.0 copy-start
  0.7 0.6 copy-done
  1.3 0.6 fusion.21
  1.9 0.0 copy-start.1
  1.9 5.3 %fusion.15 = f32[16,16,16,128]{3,0,2,1:T(8,128)} fusion(f32[16,16,1,1]{1,0,3,2:T(8,128)S(1)} %bitcast.83, f32[16,16,16,128]{3,2,1,0:T(8,128)} %param.6), kind=kOutput, calls=%fused_computation.20 | convolution fusion | flops 100663296 | bytes 4195328 | tf_op jit(solution)/shard_map/ab,ibkf->iakf/dot_general | solution.py:29
  7.2 0.0 copy-done.1
  7.2 0.0 copy-start.5
  7.2 4.1 %fusion.19 = f32[16,16,16,128]{3,0,2,1:T(8,128)} fusion(f32[16,16,1,1]{1,0,3,2:T(8,128)S(1)} %bitcast.84, f32[16,16,16,128]{3,2,1,0:T(8,128)S(1)} %copy-done.1), kind=kOutput, calls=%fused_computation.24 | convolution fusion | flops 100663296 | bytes 4195328 | tf_op jit(solution)/shard_map/ab,bjkf->ajkf/dot_general | solution.py:27
  11.4 0.0 copy-done.5
  11.4 0.6 fusion.22
  12.0 2.9 fusion.17
  14.9 0.0 copy-start.2
  14.9 0.0 copy-start.4
  14.9 3.2 fusion.9
  18.1 0.0 copy-done.2
  18.1 0.0 copy-done.4
  18.1 3.2 fusion
  21.3 2.9 fusion.12
  24.2 3.3 fusion.5
  27.5 0.0 copy-start.3
  27.5 3.8 %fusion.3 = f32[16,16,128,16]{2,3,1,0:T(8,128)} fusion(f32[16,16,1,1]{1,0,3,2:T(8,128)S(1)} %bitcast.82, f32[16,16,128,16]{2,3,1,0:T(8,128)S(1)} %fusion.5), kind=kOutput, calls=%fused_computation.7 | convolution fusion | flops 100663296 | bytes 4195328 | tf_op jit(solution)/shard_map/ab,ijbf->ijaf/dot_general | solution.py:30
  31.2 0.0 copy-done.3
  31.2 0.1 fusion.30
  31.3 0.2 reduce_window_sum.11
  31.5 0.2 select_reduce_fusion
  31.9 5.9 %fusion.2 = bf16[16,16,16,128]{3,2,1,0:T(8,128)(2,1)S(1)} fusion(f32[16,16,128,16]{2,3,1,0:T(8,128)} %fusion.3, f32[16,16,16,128]{3,0,2,1:T(8,128)} %fusion.19, f32[16,16,16,128]{3,0,2,1:T(8,128)} %fusion.15, f32[16,16,1,1]{1,0,3,2:T(8,128)S(1)} %bitcast.85, f32[16,16,16,128]{3,2,1,0:T(8,128)S(1)} %copy-done.1), kind=kOutput, calls=%fused_computation.5 | convolution fusion | flops 102760448 | bytes 9438208 | tf_op jit(solution)/shard_map/ab,ijbf->ijaf/dot_general | solution.py:30
  37.8 1.8 convolution_convert_fusion
  39.6 4.1 %all_to_all.16 = bf16[64,3,4096]{2,1,0:T(4,128)(2,1)} reshape(bf16[192,4096]{1,0:T(8,128)(2,1)} %convolution_convert_fusion) | data formatting | bytes 3145728 | tf_op jit(solution)/shard_map/all_to_all | solution.py:76
  43.7 15.4 %all-to-all-start = ((bf16[64,3,4096]{2,1,0:T(4,128)(2,1)}), bf16[64,3,4096]{2,1,0:T(4,128)(2,1)}, u32[]{:S(2)}, u32[]{:S(2)}) async-start(bf16[64,3,4096]{2,1,0:T(4,128)(2,1)} %all_to_all.16), calls=%async_computation | async-start | bytes 4194304 | tf_op jit(solution)/shard_map/all_to_all | solution.py:76
  59.1 0.1 div.10
  59.3 281.8 %psum.7 = f32[16,256]{1,0:T(8,128)S(1)} all-reduce(f32[16,256]{1,0:T(8,128)S(1)} %div.10), channel_id=1, replica_groups=mesh['dom'=12,'grp'=64] {'grp'}, use_global_device_ids=true, to_apply=%region_3.4 | all-reduce | flops 4096 | bytes 32768 | tf_op jit(solution)/shard_map/psum | solution.py:81
  341.1 1.9 collective-permute-start
  343.0 0.2 convert_element_type.22
  343.2 0.0 all-to-all-done
  343.2 3.1 all_to_all.18
  346.3 0.6 convolution_multiply_fusion
  346.9 0.7 all_to_all.19
  347.6 14.5 %all-to-all-start.1 = ((f32[64,3,128]{2,1,0:T(4,128)}), f32[64,3,128]{2,1,0:T(4,128)S(1)}, u32[]{:S(2)}, u32[]{:S(2)}) async-start(f32[64,3,128]{2,1,0:T(4,128)} %all_to_all.19), calls=%async_computation.1 | async-start | bytes 262144 | tf_op jit(solution)/shard_map/all_to_all | solution.py:79
  362.1 0.0 collective-permute-done
  362.1 0.6 slice_add_fusion
  362.7 10.5 %all-to-all-done.1 = f32[64,3,128]{2,1,0:T(4,128)S(1)} async-done(((f32[64,3,128]{2,1,0:T(4,128)}), f32[64,3,128]{2,1,0:T(4,128)S(1)}, u32[]{:S(2)}, u32[]{:S(2)}) %all-to-all-start.1) | async-done | bytes 98336 | tf_op jit(solution)/shard_map/all_to_all | solution.py:79
  373.2 0.9 fusion.23
  (6 shorter events, 0.1 us)
Async XLA Ops:
  0.6 0.7 copy-start
  1.9 5.3 %copy-start.1 = (f32[16,16,16,128]{3,2,1,0:T(8,128)S(1)}, f32[16,16,16,128]{3,2,1,0:T(8,128)}, u32[]{:S(2)}) copy-start(f32[16,16,16,128]{3,2,1,0:T(8,128)} %param.6) | copy-start | bytes 6291460
  7.2 4.1 %copy-start.5 = (f32[16]{0:T(128)S(1)}, f32[16]{0:T(128)}, u32[]{:S(2)}) copy-start(f32[16]{0:T(128)} %param.8) | copy-start | bytes 196
  14.9 3.3 copy-start.2
  14.9 3.3 copy-start.4
  27.5 3.8 %copy-start.3 = (s32[128,1]{0,1:T(1,128)S(1)}, s32[128,1]{0,1:T(1,128)}, u32[]{:S(2)}) copy-start(s32[128,1]{0,1:T(1,128)} %param.11) | copy-start | bytes 1540
  43.7 299.5 %all-to-all-start = ((bf16[64,3,4096]{2,1,0:T(4,128)(2,1)}), bf16[64,3,4096]{2,1,0:T(4,128)(2,1)}, u32[]{:S(2)}, u32[]{:S(2)}) async-start(bf16[64,3,4096]{2,1,0:T(4,128)(2,1)} %all_to_all.16), calls=%async_computation | async-start | bytes 4194304 | tf_op jit(solution)/shard_map/all_to_all | solution.py:76
  341.1 21.0 %collective-permute-start = (f32[8,256]{1,0:T(8,128)S(1)}, f32[8,256]{1,0:T(8,128)S(1)}, u32[]{:S(2)}, u32[]{:S(2)}) collective-permute-start(f32[8,256]{1,0:T(8,128)S(1)} %slice.9), channel_id=1, source_target_pairs={{704,0},{0,64},{64,128},{128,192},{192,256},{256,320},{320,384},{3... | collective-permute-start | bytes 24584 | tf_op jit(solution)/shard_map/ppermute | solution.py:12
  347.6 25.6 %all-to-all-start.1 = ((f32[64,3,128]{2,1,0:T(4,128)}), f32[64,3,128]{2,1,0:T(4,128)S(1)}, u32[]{:S(2)}, u32[]{:S(2)}) async-start(f32[64,3,128]{2,1,0:T(4,128)} %all_to_all.19), calls=%async_computation.1 | async-start | bytes 262144 | tf_op jit(solution)/shard_map/all_to_all | solution.py:79
where the time goes:
time: 375 us; the launch traced here: 374 us
  blocking collectives  282 us (75%)
  matrix products  39 us (10%)
  starting transfers between devices  31.8 us (8%)
  waiting for transfers between devices  10.5 us (3%)
  local copies, waits for them, and re-layouts  8.73 us (2%)
    psum x1, blocking collectives, body(): summed = lax.psum(density_part, 'grp')  282 us
    all_to_all x1, starting transfers between devices, body(): lax.all_to_all(outgoing, 'grp', split_axis=0, concat_axis=0, tiled=True)  15.4 us
    all_to_all x1, starting transfers between devices, body(): lax.all_to_all(products, 'grp', split_axis=0, concat_axis=0, tiled=True)  14.5 us
    dot_general x3, matrix products, filter_along(): return jnp.einsum('ab,ijbf->ijaf', matrix, field_block, precision=HIGHEST)  12.8 us
    dot_general x3, matrix products, filter_along(): return jnp.einsum('ab,ibkf->iakf', matrix, field_block, precision=HIGHEST)  11.8 us
    all_to_all x1, waiting for transfers between devices, body(): lax.all_to_all(products, 'grp', split_axis=0, concat_axis=0, tiled=True)  10.5 us
    dot_general x3, matrix products, filter_along(): return jnp.einsum('ab,bjkf->ajkf', matrix, field_block, precision=HIGHEST)  9.86 us
  transfers between devices with their start and end apart: 3, of which 1 were waited for; matrix products, arithmetic and copies ran while one was open for 0% of the time, Pallas kernels for 0%

commit v1 on v0

v1 whole, which is shorter than its diff:
```python
import functools

import jax
import jax.numpy as jnp
from jax import lax
from jax.experimental import pallas as pl
from jax.experimental.pallas import tpu as pltpu
from jax.sharding import PartitionSpec as P

F32 = jnp.float32
BF16 = jnp.bfloat16
SIDE = 16
PLANE = SIDE * SIDE
CELLS = SIDE**3
LANES = 128
CAP = 3
CHUNKS = CELLS // LANES


def split2(x):
    hi = x.astype(BF16)
    lo = (x - hi.astype(F32)).astype(BF16)
    return hi, lo


def tap_lookup(taps_ref, offset):
    out = jnp.zeros(offset.shape, F32)
    for q in range(SIDE):
        out = jnp.where(offset == q, taps_ref[q], out)
    return out


def store_split(dst, row0, mat):
    hi, lo = split2(mat)
    rows = mat.shape[0]
    dst[pl.ds(row0, rows), 0:PLANE] = hi
    dst[pl.ds(row0, rows), PLANE : 2 * PLANE] = lo
    dst[pl.ds(row0, rows), 2 * PLANE : 3 * PLANE] = hi


def stack3(x):
    hi, lo = split2(x)
    return jnp.concatenate([hi, hi, lo], axis=0)


def mm(a, b):
    return jnp.dot(a, b, preferred_element_type=F32)


def slot_of(owner_row):
    n = owner_row.shape[1]
    across = jnp.broadcast_to(owner_row.astype(F32), (n, n))
    down = across.T
    r = lax.broadcasted_iota(jnp.int32, (n, n), 0)
    c = lax.broadcasted_iota(jnp.int32, (n, n), 1)
    earlier = jnp.where((across == down) & (r < c), 1.0, 0.0)
    return jnp.sum(earlier, axis=0, keepdims=True).astype(jnp.int32)


def apply_kernel(
    groups,
    magic_ref, kinetic_ref, diag_ref, owner_ref, x_hbm, pot_hbm,
    out_ref, dens_ref,
    x_ref, pot_ref, z_ref, kin_ref, v_ref, lhs1, lhs_f, lhs_ft, lhs_k, lhs_b, sel_ref, rows_ref,
    sem_x, sem_p,
):
    copies_x, copies_p = [], []
    for q in range(4):
        part = pl.ds(q * 4, 4)
        copies_x.append(pltpu.make_async_copy(x_hbm.at[part], x_ref.at[part], sem_x.at[q]))
        copies_p.append(pltpu.make_async_copy(pot_hbm.at[part], pot_ref.at[part], sem_p.at[q]))
    for c in copies_x:
        c.start()
    for c in copies_p:
        c.start()

    half = SIDE // 2 - 1
    rr = lax.broadcasted_iota(jnp.int32, (PLANE, PLANE), 0)
    cc = lax.broadcasted_iota(jnp.int32, (PLANE, PLANE), 1)
    d_minor = lax.rem(cc, SIDE) - lax.rem(rr, SIDE)
    d_major = cc // SIDE - rr // SIDE
    same_minor = d_minor == 0
    same_major = d_major == 0
    f_minor = tap_lookup(magic_ref, d_minor + half)
    f_major = tap_lookup(magic_ref, d_major + half)
    k_minor = tap_lookup(kinetic_ref, d_minor + half)
    k_major = tap_lookup(kinetic_ref, d_major + half)
    ft_minor = tap_lookup(magic_ref, half - d_minor)
    ft_major = tap_lookup(magic_ref, half - d_major)
    store_split(lhs1, 0, f_major * f_minor)
    store_split(lhs1, PLANE, jnp.where(same_minor, k_major, 0.0) + jnp.where(same_major, k_minor, 0.0))
    store_split(lhs_f, 0, jnp.where(same_minor, f_major, 0.0))
    store_split(lhs_ft, 0, jnp.where(same_minor, ft_major, 0.0))
    store_split(lhs_k, 0, jnp.where(same_minor, k_major, 0.0))
    store_split(lhs_b, 0, ft_major * ft_minor)

    owner = owner_ref[...]
    column = slot_of(owner) * groups + owner
    ri = lax.broadcasted_iota(jnp.int32, (CAP * groups, LANES), 0)
    sel_ref[...] = jnp.where(ri == column, 1.0, 0.0).astype(BF16)

    def pair(ref, axis, p):
        if axis == 0:
            a, b = ref[2 * p], ref[2 * p + 1]
        else:
            a, b = ref[:, 2 * p], ref[:, 2 * p + 1]
        return jnp.concatenate([a.reshape(PLANE, LANES), b.reshape(PLANE, LANES)], axis=1)

    def halves(y):
        return [y[:, h * LANES : (h + 1) * LANES].reshape(SIDE, SIDE, LANES) for h in (0, 1)]

    for c in copies_x:
        c.wait()

    def phase_a(p, carry):
        y = mm(lhs1[...], stack3(pair(x_ref, 0, p)))
        for h, (z, k) in enumerate(zip(halves(y[:PLANE]), halves(y[PLANE:]))):
            z_ref[2 * p + h] = z
            kin_ref[2 * p + h] = k
        return carry

    lax.fori_loop(0, SIDE // 2, phase_a, 0)
    for c in copies_p:
        c.wait()

    def phase_b(p, carry):
        r = mm(lhs_f[...], stack3(pair(z_ref, 1, p)))
        w = r * pair(pot_ref, 1, p)
        v = mm(lhs_ft[...], stack3(w))
        k = mm(lhs_k[...], stack3(pair(x_ref, 1, p)))
        for h, (rh, vh, kh) in enumerate(zip(halves(r), halves(v), halves(k))):
            z_ref[:, 2 * p + h] = rh
            v_ref[:, 2 * p + h] = vh
            kin_ref[:, 2 * p + h] += kh
        return carry

    lax.fori_loop(0, SIDE // 2, phase_b, 0)

    diag = diag_ref[...] * (1.0 / (LANES * groups))
    ones = jnp.ones((8, 2 * LANES), BF16)
    nt = (((1,), (1,)), ((), ()))

    def phase_c(p, carry):
        g = mm(lhs_b[...], stack3(pair(v_ref, 0, p))) + pair(kin_ref, 0, p)
        gb = g.astype(BF16)
        for h in (0, 1):
            i = 2 * p + h
            r = z_ref[i].reshape(PLANE, LANES)
            hi, lo = split2(diag * r * r)
            d = lax.dot_general(ones, jnp.concatenate([hi, lo], axis=1), nt, preferred_element_type=F32)
            dens_ref[pl.ds(i, 1), :] = d[0:1]
            sent = lax.dot_general(
                sel_ref[...], gb[:, h * LANES : (h + 1) * LANES], nt, preferred_element_type=F32
            )
            for s in range(CAP):
                for c in (0, 1):
                    rows_ref[pl.ds(s * CHUNKS + 2 * i + c, groups, stride=CAP * CHUNKS), :] = sent[
                        s * groups : (s + 1) * groups, c * LANES : (c + 1) * LANES
                    ]
        return carry

    lax.fori_loop(0, SIDE // 2, phase_c, 0)

    def pack(g, carry):
        out_ref[g] = rows_ref[pl.ds(g * CAP * CHUNKS, CAP * CHUNKS), :].astype(BF16)
        return carry

    lax.fori_loop(0, groups, pack, 0, unroll=4)


def run_apply(support, potential, magic_taps, kinetic_taps, kernel_diag, owners, groups):
    vm = pl.BlockSpec(memory_space=pltpu.VMEM)
    sm = pl.BlockSpec(memory_space=pltpu.SMEM)
    hbm = pl.BlockSpec(memory_space=pl.ANY)
    box = (SIDE, SIDE, SIDE, LANES)
    lhs = pltpu.VMEM((PLANE, 3 * PLANE), BF16)

    return pl.pallas_call(
        functools.partial(apply_kernel, groups),
        out_shape=(
            jax.ShapeDtypeStruct((groups, CAP * CHUNKS, LANES), BF16),
            jax.ShapeDtypeStruct((SIDE, PLANE), F32),
        ),
        in_specs=[sm, sm, vm, vm, hbm, hbm],
        out_specs=(vm, vm),
        scratch_shapes=[
            pltpu.VMEM(box, F32), pltpu.VMEM(box, F32), pltpu.VMEM(box, F32), pltpu.VMEM(box, F32), pltpu.VMEM(box, F32),
            pltpu.VMEM((2 * PLANE, 3 * PLANE), BF16), lhs, lhs, lhs, lhs,
            pltpu.VMEM((CAP * groups, LANES), BF16),
            pltpu.VMEM((groups * CAP * CHUNKS, LANES), F32),
            pltpu.SemaphoreType.DMA((4,)), pltpu.SemaphoreType.DMA((4,)),
        ],
        compiler_params=pltpu.CompilerParams(vmem_limit_bytes=48 * 1024 * 1024),
    )(magic_taps, kinetic_taps, kernel_diag.reshape(1, LANES), owners.reshape(1, LANES), support, potential)


def margin_kernel(groups, recv_ref, coef_ref, scale_ref, out_ref, rows_ref):
    def unpack(g, carry):
        rows_ref[pl.ds(g * CAP * CHUNKS, CAP * CHUNKS), :] = recv_ref[g].astype(F32)
        return carry

    lax.fori_loop(0, groups, unpack, 0, unroll=4)

    def step(i, acc):
        parts = []
        for s in range(CAP):
            cols = [
                rows_ref[pl.ds(s * CHUNKS + 2 * i + c, groups, stride=CAP * CHUNKS), :] for c in (0, 1)
            ]
            parts.append(jnp.concatenate(cols, axis=1))
        lhs = jnp.concatenate(parts, axis=0).astype(BF16)
        rhs = coef_ref[pl.ds(pl.multiple_of(i * PLANE, PLANE), PLANE), :].astype(BF16)
        return acc + mm(lhs, rhs)

    acc = lax.fori_loop(0, SIDE, step, jnp.zeros((CAP * groups, LANES), F32))
    acc = acc * (scale_ref[...] * (1.0 / float(SIDE) ** 1.5))
    for s in range(CAP):
        out_ref[pl.ds(s, groups, stride=4), :] = acc[s * groups : (s + 1) * groups]
    out_ref[pl.ds(CAP, groups, stride=4), :] = jnp.zeros((groups, LANES), F32)


def run_margin(received, owned, kernel_diag, groups):

    vm = pl.BlockSpec(memory_space=pltpu.VMEM)
    return pl.pallas_call(
        functools.partial(margin_kernel, groups),
        out_shape=jax.ShapeDtypeStruct((groups * 4, LANES), F32),
        in_specs=[vm, vm, vm],
        out_specs=vm,
        scratch_shapes=[pltpu.VMEM((groups * CAP * CHUNKS, LANES), F32)],
        compiler_params=pltpu.CompilerParams(vmem_limit_bytes=32 * 1024 * 1024),
    )(received, owned, kernel_diag.reshape(1, LANES))


def gather_kernel(owner_ref, ret_ref, out_ref):
    owner = owner_ref[...]
    column = owner * 4 + slot_of(owner)
    n = ret_ref.shape[0]
    ri = lax.broadcasted_iota(jnp.int32, (n, LANES), 0)
    onehot = jnp.where(ri == column, 1.0, 0.0).T.astype(BF16)
    x = ret_ref[...]
    hi, mid = split2(x)
    lo = (x - hi.astype(F32) - mid.astype(F32)).astype(BF16)
    out_ref[...] = mm(onehot, hi) + (mm(onehot, mid) + mm(onehot, lo))


def run_gather(owners, returned):
    vm = pl.BlockSpec(memory_space=pltpu.VMEM)
    return pl.pallas_call(
        gather_kernel,
        out_shape=jax.ShapeDtypeStruct((LANES, LANES), F32),
        in_specs=[vm, vm],
        out_specs=vm,
    )(owners.reshape(1, LANES), returned)


def body(support, potential, magic_taps, kinetic_taps, kernel_diag, owners):
    groups = lax.axis_size("grp")
    domains = lax.axis_size("dom")
    outgoing, part = run_apply(support, potential, magic_taps, kinetic_taps, kernel_diag, owners, groups)
    received = lax.all_to_all(outgoing, "grp", split_axis=0, concat_axis=0, tiled=True)
    distance = 1
    while distance < groups:
        part = part + lax.ppermute(part, "grp", [(i, i ^ distance) for i in range(groups)])
        distance *= 2
    half = SIDE // 2
    upper = lax.ppermute(part[half:], "dom", [(i, (i + 1) % domains) for i in range(domains)])
    density = part[:half] + upper
    products = run_margin(received, support.reshape(CELLS, LANES), kernel_diag, groups)
    returned = lax.all_to_all(
        products.reshape(groups, 4, LANES), "grp", split_axis=0, concat_axis=0, tiled=True
    )
    margin = run_gather(owners, returned.reshape(groups * 4, LANES))
    return margin, density


def solution(mesh):
    return jax.shard_map(
        body,
        mesh=mesh,
        in_specs=(
            P(None, None, None, ("dom", "grp")),
            P(None, None, None, ("dom", "grp")),
            P(),
            P(),
            P(("dom", "grp")),
            P(("dom", "grp"), None),
        ),
        out_specs=(P(("dom", "grp"), None), P("dom", None)),
        check_vma=False,
    )
```

time: 375 us -> 121 us (0.32)
  blocking collectives: 282 us -> 0 us
  matrix products: 39 us -> 0 us
  Pallas kernels: 0 us -> 26.1 us
  waiting for transfers between devices: 10.5 us -> 35.1 us
  starting transfers between devices: 31.8 us -> 49.6 us
    psum x1 -> x0, blocking collectives: 282 us -> none  [body(): summed = lax.psum(density_part, 'grp')]
    dot_general x14 -> x0, matrix products: 39 us -> none  [the longest x3 12.8 us: filter_along(): return jnp.einsum('ab,ijbf->ijaf', matrix, field_block, precision=HIGHEST)]
    ppermute x1 -> x7, waiting for transfers between devices: 0.01 us -> 34.3 us  [the longest x6 24.6 us: body(): lax.ppermute(part, 'grp', [(i, i ^ distance) for i in range(groups)])]
    pallas_call x0 -> x3, Pallas kernels: none -> 26.1 us  [the longest x1 18.2 us: run_apply(): pl.pallas_call(functools.partial(apply_kernel, groups), out_shape=(jax.Sh...]
    ppermute x1 -> x7, starting transfers between devices: 1.91 us -> 24.8 us  [the longest x6 22.9 us: body(): lax.ppermute(part, 'grp', [(i, i ^ distance) for i in range(groups)])]
    all_to_all x1, waiting for transfers between devices: 10.5 us -> 0.01 us  [body(): lax.all_to_all(products.reshape(groups, 4, LANES), 'grp', split_axis=0, c...]
    all_to_all x4 -> x0, local copies, waits for them, and re-layouts: 7.96 us -> none  [the longest x2 7.22 us: body(): lax.all_to_all(outgoing, 'grp', split_axis=0, concat_axis=0, tiled=True)]
    unnamed x12 -> x20, local copies, waits for them, and re-layouts: 0.67 us -> 7.57 us
  transfers between devices with their start and end apart: 3 -> 9, of which waited for: 1 -> 7; matrix products, arithmetic and copies ran while one was open for 0% -> 1% of each run, Pallas kernels for 0% -> 5%
where the time goes in v1:
time: 121 us; the launch traced here: 120 us
  starting transfers between devices  49.6 us (41%)
  waiting for transfers between devices  35.1 us (29%)
  Pallas kernels  26.1 us (22%)
  local copies, waits for them, and re-layouts  7.58 us (6%)
    ppermute x6, waiting for transfers between devices, body(): lax.ppermute(part, 'grp', [(i, i ^ distance) for i in range(groups)])  24.6 us
    ppermute x6, starting transfers between devices, body(): lax.ppermute(part, 'grp', [(i, i ^ distance) for i in range(groups)])  22.9 us
    pallas_call x1, Pallas kernels, run_apply(): pl.pallas_call(functools.partial(apply_kernel, groups), out_shape=(jax.Sh...  18.2 us
    all_to_all x1, starting transfers between devices, body(): lax.all_to_all(outgoing, 'grp', split_axis=0, concat_axis=0, tiled=True)  15.5 us
    ppermute x1, waiting for transfers between devices, body(): lax.ppermute(part[half:], 'dom', [(i, (i + 1) % domains) for i in range(d...  9.69 us
    all_to_all x1, starting transfers between devices, body(): lax.all_to_all(products.reshape(groups, 4, LANES), 'grp', split_axis=0, c...  9.21 us
    unnamed x20, local copies, waits for them, and re-layouts  7.57 us
    pallas_call x1, Pallas kernels, run_margin(): pl.pallas_call(functools.partial(margin_kernel, groups), out_shape=jax.Sh...  6.05 us
  transfers between devices with their start and end apart: 9, of which 7 were waited for; matrix products, arithmetic and copies ran while one was open for 1% of the time, Pallas kernels for 5%

profile of v1, /device:TPU:1, one launch (start us, length us, event | category | flops | bytes accessed | tf_op | source)
XLA Modules:
  0.0 119.8 jit_solution(2026781392995912927)
XLA Ops:
  0.6 0.0 copy-start
  0.6 1.6 %copy-done = f32[16,16,16,128]{3,2,1,0:T(8,128)S(1)} copy-done((f32[16,16,16,128]{3,2,1,0:T(8,128)S(1)}, f32[16,16,16,128]{3,2,1,0:T(8,128)}, u32[]{:S(2)}) %copy-start) | copy-done | bytes 2097176
  2.2 0.0 copy-start.2
  2.2 1.6 %copy-done.2 = f32[16,16,16,128]{3,2,1,0:T(8,128)S(1)} copy-done((f32[16,16,16,128]{3,2,1,0:T(8,128)S(1)}, f32[16,16,16,128]{3,2,1,0:T(8,128)}, u32[]{:S(2)}) %copy-start.2) | copy-done | bytes 2097176
  3.8 0.0 copy-start.4
  3.8 0.7 copy-done.4
  4.5 0.0 copy-start.6
  4.5 0.7 copy-done.6
  5.1 0.0 copy-start.7
  5.1 0.7 copy-done.7
  5.8 0.0 copy-start.8
  5.8 0.7 copy-done.8
  6.4 18.2 %shard_map.77 = (bf16[64,96,128]{2,1,0:T(8,128)(2,1)S(1)}, f32[16,256]{1,0:T(8,128)S(1)}) custom-call(f32[16]{0:T(128)S(1)} %copy-done.7, f32[16]{0:T(128)S(1)} %copy-done.8, f32[1,128]{1,0:T(1,128)S(1)} %bitcast.6, s32[1,128]{1,0:T(1,128)S(1)} %bitcast.9, f32[16,16,16,128]{3,2,1,0:T(8,128)S(1)} %copy-done, f32[16,16,16,128]{3,2,1,0:T(8,128)S(1)} %copy-done.2), custom_call_target="tpu_custom_call" | custom-call | tf_op jit(solution)/shard_map/pallas_call | solution.py:178
  24.6 0.0 copy-start.3
  24.6 1.1 copy-done.3
  25.7 0.0 copy-start.1
  25.7 0.0 copy-start.5
  25.7 15.5 %all-to-all-start = ((bf16[64,96,128]{2,1,0:T(8,128)(2,1)}), bf16[64,96,128]{2,1,0:T(8,128)(2,1)}, u32[]{:S(2)}, u32[]{:S(2)}) async-start(bf16[64,96,128]{2,1,0:T(8,128)(2,1)} %copy-done.3), calls=%async_computation | async-start | bytes 3145728 | tf_op jit(solution)/shard_map/all_to_all | solution.py:261
  41.3 2.5 %collective-permute-start = (f32[16,256]{1,0:T(8,128)S(1)}, f32[16,256]{1,0:T(8,128)S(1)}, u32[]{:S(2)}, u32[]{:S(2)}) collective-permute-start(f32[16,256]{1,0:T(8,128)S(1)} %get-tuple-element.5), channel_id=1, source_target_pairs={{0,1},{1,0},{2,3},{3,2},{4,5},{5,4},{6,7},{7,6},{8,9},{9,8},{10,11... | collective-permute-start | bytes 49160 | tf_op jit(solution)/shard_map/ppermute | solution.py:264
  43.8 0.8 collective-permute-done
  44.6 3.0 %collective-permute-start.1 = (f32[16,256]{1,0:T(8,128)S(1)}, f32[16,256]{1,0:T(8,128)S(1)}, u32[]{:S(2)}, u32[]{:S(2)}) collective-permute-start(f32[16,256]{1,0:T(8,128)S(1)} %add.21), channel_id=1, source_target_pairs={{0,2},{1,3},{2,0},{3,1},{4,6},{5,7},{6,4},{7,5},{8,10},{9,11},{10,... | collective-permute-start | bytes 49160 | tf_op jit(solution)/shard_map/ppermute | solution.py:264
  47.7 1.9 %collective-permute-done.1 = f32[16,256]{1,0:T(8,128)S(1)} collective-permute-done((f32[16,256]{1,0:T(8,128)S(1)}, f32[16,256]{1,0:T(8,128)S(1)}, u32[]{:S(2)}, u32[]{:S(2)}) %collective-permute-start.1) | collective-permute-done | bytes 16416 | tf_op jit(solution)/shard_map/ppermute | solution.py:264
  49.6 4.9 %collective-permute-start.2 = (f32[16,256]{1,0:T(8,128)S(1)}, f32[16,256]{1,0:T(8,128)S(1)}, u32[]{:S(2)}, u32[]{:S(2)}) collective-permute-start(f32[16,256]{1,0:T(8,128)S(1)} %add.22), channel_id=1, source_target_pairs={{0,4},{1,5},{2,6},{3,7},{4,0},{5,1},{6,2},{7,3},{8,12},{9,13},{10,... | collective-permute-start | bytes 49160 | tf_op jit(solution)/shard_map/ppermute | solution.py:264
  54.5 1.8 %collective-permute-done.2 = f32[16,256]{1,0:T(8,128)S(1)} collective-permute-done((f32[16,256]{1,0:T(8,128)S(1)}, f32[16,256]{1,0:T(8,128)S(1)}, u32[]{:S(2)}, u32[]{:S(2)}) %collective-permute-start.2) | collective-permute-done | bytes 16416 | tf_op jit(solution)/shard_map/ppermute | solution.py:264
  56.3 2.8 %collective-permute-start.3 = (f32[16,256]{1,0:T(8,128)S(1)}, f32[16,256]{1,0:T(8,128)S(1)}, u32[]{:S(2)}, u32[]{:S(2)}) collective-permute-start(f32[16,256]{1,0:T(8,128)S(1)} %add.23), channel_id=1, source_target_pairs={{0,8},{1,9},{2,10},{3,11},{4,12},{5,13},{6,14},{7,15},{8,0},{9,1},... | collective-permute-start | bytes 49160 | tf_op jit(solution)/shard_map/ppermute | solution.py:264
  59.1 17.9 %collective-permute-done.3 = f32[16,256]{1,0:T(8,128)S(1)} collective-permute-done((f32[16,256]{1,0:T(8,128)S(1)}, f32[16,256]{1,0:T(8,128)S(1)}, u32[]{:S(2)}, u32[]{:S(2)}) %collective-permute-start.3) | collective-permute-done | bytes 16416 | tf_op jit(solution)/shard_map/ppermute | solution.py:264
  77.1 2.4 %collective-permute-start.4 = (f32[16,256]{1,0:T(8,128)S(1)}, f32[16,256]{1,0:T(8,128)S(1)}, u32[]{:S(2)}, u32[]{:S(2)}) collective-permute-start(f32[16,256]{1,0:T(8,128)S(1)} %add.24), channel_id=1, source_target_pairs={{0,16},{1,17},{2,18},{3,19},{4,20},{5,21},{6,22},{7,23},{8,24},{9,... | collective-permute-start | bytes 49160 | tf_op jit(solution)/shard_map/ppermute | solution.py:264
  79.5 0.9 all-to-all-done.recv_ref
  80.3 0.0 copy-done.1
  80.3 0.0 copy-done.5
  80.3 6.1 %shard_map.78 = f32[256,128]{1,0:T(8,128)} custom-call(bf16[64,96,128]{2,1,0:T(8,128)(2,1)} %all-to-all-done.recv_ref, f32[4096,128]{1,0:T(8,128)S(1)} %bitcast.5, f32[1,128]{1,0:T(1,128)S(1)} %bitcast.7), custom_call_target="tpu_custom_call" | custom-call | tf_op jit(solution)/shard_map/pallas_call | solution.py:225
  86.4 9.2 %all-to-all-start.1 = ((f32[64,4,128]{2,1,0:T(4,128)}), f32[64,4,128]{2,1,0:T(4,128)S(1)}, u32[]{:S(2)}, u32[]{:S(2)}) async-start(f32[64,4,128]{2,1,0:T(4,128)} %bitcast.3), calls=%async_computation.1 | async-start | bytes 262144 | tf_op jit(solution)/shard_map/all_to_all | solution.py:270
  95.6 0.0 collective-permute-done.4
  95.6 7.3 %collective-permute-start.5 = (f32[16,256]{1,0:T(8,128)S(1)}, f32[16,256]{1,0:T(8,128)S(1)}, u32[]{:S(2)}, u32[]{:S(2)}) collective-permute-start(f32[16,256]{1,0:T(8,128)S(1)} %add.25), channel_id=1, source_target_pairs={{0,32},{1,33},{2,34},{3,35},{4,36},{5,37},{6,38},{7,39},{8,40},{9,... | collective-permute-start | bytes 49160 | tf_op jit(solution)/shard_map/ppermute | solution.py:264
  102.9 2.1 %collective-permute-done.5 = f32[16,256]{1,0:T(8,128)S(1)} collective-permute-done((f32[16,256]{1,0:T(8,128)S(1)}, f32[16,256]{1,0:T(8,128)S(1)}, u32[]{:S(2)}, u32[]{:S(2)}) %collective-permute-start.5) | collective-permute-done | bytes 16416 | tf_op jit(solution)/shard_map/ppermute | solution.py:264
  105.0 1.9 %collective-permute-start.6 = (f32[8,256]{1,0:T(8,128)S(1)}, f32[8,256]{1,0:T(8,128)S(1)}, u32[]{:S(2)}, u32[]{:S(2)}) collective-permute-start(f32[8,256]{1,0:T(8,128)S(1)} %slice.9), channel_id=1, source_target_pairs={{0,64},{64,128},{128,192},{192,256},{256,320},{320,384},{384,448},... | collective-permute-start | bytes 24584 | tf_op jit(solution)/shard_map/ppermute | solution.py:267
  106.9 9.7 %collective-permute-done.6 = f32[8,256]{1,0:T(8,128)S(1)} collective-permute-done((f32[8,256]{1,0:T(8,128)S(1)}, f32[8,256]{1,0:T(8,128)S(1)}, u32[]{:S(2)}, u32[]{:S(2)}) %collective-permute-start.6) | collective-permute-done | bytes 8224 | tf_op jit(solution)/shard_map/ppermute | solution.py:267
  116.6 0.6 slice_add_fusion
  117.2 0.0 all-to-all-done.1
  117.2 0.0 copy-start.9
  117.2 0.6 copy-done.9
  117.9 1.9 %shard_map.79 = f32[128,128]{1,0:T(8,128)} custom-call(s32[1,128]{1,0:T(1,128)} %bitcast.8, f32[256,128]{1,0:T(8,128)} %bitcast.10), custom_call_target="tpu_custom_call" | custom-call | tf_op jit(solution)/shard_map/pallas_call | solution.py:249
  (7 shorter events, 0.0 us)
Async XLA Ops:
  0.6 1.6 %copy-start = (f32[16,16,16,128]{3,2,1,0:T(8,128)S(1)}, f32[16,16,16,128]{3,2,1,0:T(8,128)}, u32[]{:S(2)}) copy-start(f32[16,16,16,128]{3,2,1,0:T(8,128)} %x_hbm.1) | copy-start | bytes 6291460
  2.2 1.6 %copy-start.2 = (f32[16,16,16,128]{3,2,1,0:T(8,128)S(1)}, f32[16,16,16,128]{3,2,1,0:T(8,128)}, u32[]{:S(2)}) copy-start(f32[16,16,16,128]{3,2,1,0:T(8,128)} %pot_hbm.1) | copy-start | bytes 6291460
  3.8 0.7 copy-start.4
  4.5 0.7 copy-start.6
  5.1 0.7 copy-start.7
  5.8 0.7 copy-start.8
  24.6 1.1 copy-start.3
  25.7 54.6 %copy-start.1 = (f32[16,16,16,128]{3,2,1,0:T(8,128)S(1)}, f32[16,16,16,128]{3,2,1,0:T(8,128)}, u32[]{:S(2)}) copy-start(f32[16,16,16,128]{3,2,1,0:T(8,128)} %x_hbm.1) | copy-start | bytes 6291460
  25.7 54.6 %copy-start.5 = (f32[128]{0:T(128)S(1)}, f32[128]{0:T(128)}, u32[]{:S(2)}) copy-start(f32[128]{0:T(128)} %param.10) | copy-start | bytes 1540
  25.7 54.6 %all-to-all-start = ((bf16[64,96,128]{2,1,0:T(8,128)(2,1)}), bf16[64,96,128]{2,1,0:T(8,128)(2,1)}, u32[]{:S(2)}, u32[]{:S(2)}) async-start(bf16[64,96,128]{2,1,0:T(8,128)(2,1)} %copy-done.3), calls=%async_computation | async-start | bytes 3145728 | tf_op jit(solution)/shard_map/all_to_all | solution.py:261
  41.3 3.4 %collective-permute-start = (f32[16,256]{1,0:T(8,128)S(1)}, f32[16,256]{1,0:T(8,128)S(1)}, u32[]{:S(2)}, u32[]{:S(2)}) collective-permute-start(f32[16,256]{1,0:T(8,128)S(1)} %get-tuple-element.5), channel_id=1, source_target_pairs={{0,1},{1,0},{2,3},{3,2},{4,5},{5,4},{6,7},{7,6},{8,9},{9,8},{10,11... | collective-permute-start | bytes 49160 | tf_op jit(solution)/shard_map/ppermute | solution.py:264
  44.6 5.0 %collective-permute-start.1 = (f32[16,256]{1,0:T(8,128)S(1)}, f32[16,256]{1,0:T(8,128)S(1)}, u32[]{:S(2)}, u32[]{:S(2)}) collective-permute-start(f32[16,256]{1,0:T(8,128)S(1)} %add.21), channel_id=1, source_target_pairs={{0,2},{1,3},{2,0},{3,1},{4,6},{5,7},{6,4},{7,5},{8,10},{9,11},{10,... | collective-permute-start | bytes 49160 | tf_op jit(solution)/shard_map/ppermute | solution.py:264
  49.6 6.7 %collective-permute-start.2 = (f32[16,256]{1,0:T(8,128)S(1)}, f32[16,256]{1,0:T(8,128)S(1)}, u32[]{:S(2)}, u32[]{:S(2)}) collective-permute-start(f32[16,256]{1,0:T(8,128)S(1)} %add.22), channel_id=1, source_target_pairs={{0,4},{1,5},{2,6},{3,7},{4,0},{5,1},{6,2},{7,3},{8,12},{9,13},{10,... | collective-permute-start | bytes 49160 | tf_op jit(solution)/shard_map/ppermute | solution.py:264
  56.3 20.7 %collective-permute-start.3 = (f32[16,256]{1,0:T(8,128)S(1)}, f32[16,256]{1,0:T(8,128)S(1)}, u32[]{:S(2)}, u32[]{:S(2)}) collective-permute-start(f32[16,256]{1,0:T(8,128)S(1)} %add.23), channel_id=1, source_target_pairs={{0,8},{1,9},{2,10},{3,11},{4,12},{5,13},{6,14},{7,15},{8,0},{9,1},... | collective-permute-start | bytes 49160 | tf_op jit(solution)/shard_map/ppermute | solution.py:264
  77.1 18.5 %collective-permute-start.4 = (f32[16,256]{1,0:T(8,128)S(1)}, f32[16,256]{1,0:T(8,128)S(1)}, u32[]{:S(2)}, u32[]{:S(2)}) collective-permute-start(f32[16,256]{1,0:T(8,128)S(1)} %add.24), channel_id=1, source_target_pairs={{0,16},{1,17},{2,18},{3,19},{4,20},{5,21},{6,22},{7,23},{8,24},{9,... | collective-permute-start | bytes 49160 | tf_op jit(solution)/shard_map/ppermute | solution.py:264
  86.4 30.8 %all-to-all-start.1 = ((f32[64,4,128]{2,1,0:T(4,128)}), f32[64,4,128]{2,1,0:T(4,128)S(1)}, u32[]{:S(2)}, u32[]{:S(2)}) async-start(f32[64,4,128]{2,1,0:T(4,128)} %bitcast.3), calls=%async_computation.1 | async-start | bytes 262144 | tf_op jit(solution)/shard_map/all_to_all | solution.py:270
  95.6 9.4 %collective-permute-start.5 = (f32[16,256]{1,0:T(8,128)S(1)}, f32[16,256]{1,0:T(8,128)S(1)}, u32[]{:S(2)}, u32[]{:S(2)}) collective-permute-start(f32[16,256]{1,0:T(8,128)S(1)} %add.25), channel_id=1, source_target_pairs={{0,32},{1,33},{2,34},{3,35},{4,36},{5,37},{6,38},{7,39},{8,40},{9,... | collective-permute-start | bytes 49160 | tf_op jit(solution)/shard_map/ppermute | solution.py:264
  105.0 11.6 %collective-permute-start.6 = (f32[8,256]{1,0:T(8,128)S(1)}, f32[8,256]{1,0:T(8,128)S(1)}, u32[]{:S(2)}, u32[]{:S(2)}) collective-permute-start(f32[8,256]{1,0:T(8,128)S(1)} %slice.9), channel_id=1, source_target_pairs={{0,64},{64,128},{128,192},{192,256},{256,320},{320,384},{384,448},... | collective-permute-start | bytes 24584 | tf_op jit(solution)/shard_map/ppermute | solution.py:267
  117.2 0.6 copy-start.9

commit v2 on v1

v2 whole, which is shorter than its diff:
```python
import functools

import jax
import jax.numpy as jnp
from jax import lax
from jax.experimental import pallas as pl
from jax.experimental.pallas import tpu as pltpu
from jax.sharding import PartitionSpec as P

F32 = jnp.float32
BF16 = jnp.bfloat16
SIDE = 16
HALF = SIDE // 2
PLANE = SIDE * SIDE
CELLS = SIDE**3
LANES = 128
CAP = 3
CHUNKS = CELLS // LANES
BLOCK = CAP * CHUNKS
BACK = 8
NT = (((1,), (1,)), ((), ()))

VM = pl.BlockSpec(memory_space=pltpu.VMEM)
HBM = pl.BlockSpec(memory_space=pltpu.HBM)


def split2(x):
    hi = x.astype(BF16)
    lo = (x - hi.astype(F32)).astype(BF16)
    return hi, lo


def mm(a, b):
    return jnp.dot(a, b, preferred_element_type=F32)


def tap_lookup(taps_ref, offset):
    out = jnp.zeros(offset.shape, F32)
    for q in range(SIDE):
        out = jnp.where(offset == q, taps_ref[q], out)
    return out


def stack3(x):
    hi, lo = split2(x)
    return jnp.concatenate([hi, hi, lo], axis=0)


def slot_of(owner_row):
    n = owner_row.shape[1]
    across = jnp.broadcast_to(owner_row.astype(F32), (n, n))
    down = across.T
    r = lax.broadcasted_iota(jnp.int32, (n, n), 0)
    c = lax.broadcasted_iota(jnp.int32, (n, n), 1)
    earlier = jnp.where((across == down) & (r < c), 1.0, 0.0)
    return jnp.sum(earlier, axis=0, keepdims=True).astype(jnp.int32)


def build_plane_matrices(magic, kinetic, pat_ref, lhs1, lhs_b):
    half = SIDE // 2 - 1
    a = lax.broadcasted_iota(jnp.int32, (SIDE, PLANE), 0)
    c = lax.broadcasted_iota(jnp.int32, (SIDE, PLANE), 1)
    minor = jnp.bitwise_and(c, SIDE - 1) - a
    major = jnp.right_shift(c, 4) - a
    f_minor = tap_lookup(magic, minor + half)
    k_minor = tap_lookup(kinetic, minor + half)
    ft_minor = tap_lookup(magic, half - minor)
    pat_ref[0] = tap_lookup(magic, major + half)
    pat_ref[1] = tap_lookup(kinetic, major + half)
    pat_ref[2] = tap_lookup(magic, half - major)
    same_minor = minor == 0
    lane_major = jnp.right_shift(c, 4)

    def put(dst, row, mat, third):
        hi, lo = split2(mat)
        dst[pl.ds(row, SIDE), 0:PLANE] = hi
        dst[pl.ds(row, SIDE), PLANE : 2 * PLANE] = lo
        if third:
            dst[pl.ds(row, SIDE), 2 * PLANE : 3 * PLANE] = hi

    def rows(g, carry):
        r = pl.multiple_of(g * SIDE, SIDE)
        fm = pat_ref[0, pl.ds(g, 1), :]
        km = pat_ref[1, pl.ds(g, 1), :]
        bm = pat_ref[2, pl.ds(g, 1), :]
        put(lhs1, r, fm * f_minor, False)
        put(lhs1, r + PLANE, jnp.where(same_minor, km, 0.0) + jnp.where(lane_major == g, k_minor, 0.0), False)
        put(lhs_b, r, bm * ft_minor, True)
        return carry

    lax.fori_loop(0, SIDE, rows, 0)


def build_side_matrix(taps, lhs, transposed, double):
    n = SIDE * HALF
    half = SIDE // 2 - 1
    r = lax.broadcasted_iota(jnp.int32, (n, n), 0)
    c = lax.broadcasted_iota(jnp.int32, (n, n), 1)
    delta = jnp.right_shift(c, 3) - jnp.right_shift(r, 3)
    offset = half - delta if transposed else delta + half
    same = jnp.bitwise_and(r, HALF - 1) == jnp.bitwise_and(c, HALF - 1)
    hi, lo = split2(tap_lookup(taps, jnp.where(same, offset, -1)))
    lhs[0:n, 0:n] = hi
    if not double:
        lhs[0:n, n : 2 * n] = lo
        return
    lhs[0:n, n : 2 * n] = hi
    lhs[n : 2 * n, 0:n] = lo
    lhs[n : 2 * n, n : 2 * n] = lo


def apply_kernel(
    groups,
    magic_hbm, kinetic_hbm, diag_hbm, owner_hbm, x_hbm, pot_hbm,
    out_hbm, dens_ref,
    x_ref, pot_ref, z_ref, kin_ref, v_ref,
    pat_ref, lhs1, lhs_b, lhs_f, lhs_ft, lhs_k, sel_ref, rows_ref, acc_ref, stage_ref, grad_ref,
    magic, kinetic, diag_ref, owner_ref,
    sem_s, sem_x, sem_p, sem_o,
):
    small = [
        pltpu.make_async_copy(src, dst, sem_s.at[q])
        for q, (src, dst) in enumerate(
            [(magic_hbm, magic), (kinetic_hbm, kinetic), (diag_hbm, diag_ref), (owner_hbm, owner_ref)]
        )
    ]
    parts = 4
    width = SIDE // parts
    copies_x, copies_p = [], []
    for q in range(parts):
        part = pl.ds(q * width, width)
        copies_x.append(pltpu.make_async_copy(x_hbm.at[part], x_ref.at[part], sem_x.at[q]))
        copies_p.append(pltpu.make_async_copy(pot_hbm.at[part], pot_ref.at[part], sem_p.at[q]))
    for c in small + copies_x + copies_p:
        c.start()
    for c in small:
        c.wait()

    build_plane_matrices(magic, kinetic, pat_ref, lhs1, lhs_b)
    build_side_matrix(magic, lhs_f, False, True)
    build_side_matrix(magic, lhs_ft, True, True)
    build_side_matrix(kinetic, lhs_k, False, False)
    owner = owner_ref[...]
    column = slot_of(owner) * groups + owner
    ri = lax.broadcasted_iota(jnp.int32, (CAP * groups, LANES), 0)
    sel_ref[...] = jnp.where(ri == column, 1.0, 0.0).astype(BF16)
    acc_ref[...] = jnp.zeros_like(acc_ref)

    def planes(ref, p):
        a, b = ref[2 * p], ref[2 * p + 1]
        return jnp.concatenate([a.reshape(PLANE, LANES), b.reshape(PLANE, LANES)], axis=1)

    def phase_a(p, carry):
        x = planes(x_ref, p).astype(BF16)
        y = mm(lhs1[...], jnp.concatenate([x, x], axis=0))
        for h in (0, 1):
            cols = slice(h * LANES, (h + 1) * LANES)
            z_ref[2 * p + h] = y[:PLANE, cols].reshape(SIDE, SIDE, LANES)
            kin_ref[2 * p + h] = y[PLANE:, cols].reshape(SIDE, SIDE, LANES)
        return carry

    for q in range(parts):
        copies_x[q].wait()
        lax.fori_loop(q * width // 2, (q + 1) * width // 2, phase_a, 0, unroll=True)
    for c in copies_p:
        c.wait()

    side = SIDE * HALF
    diag = diag_ref[...] * (1.0 / (LANES * groups))
    diag2 = jnp.concatenate([diag, diag], axis=1)
    ones = jnp.ones((2 * LANES, LANES), BF16)
    lane = lax.broadcasted_iota(jnp.int32, (HALF, LANES), 1)
    sub = lax.broadcasted_iota(jnp.int32, (HALF, LANES), 0)

    def column_pair(ref, j):
        s = ref[:, j]
        return jnp.concatenate(
            [s[:, :HALF].reshape(side, LANES), s[:, HALF:].reshape(side, LANES)], axis=1
        )

    def along_i(lhs, x):
        hi, lo = split2(x)
        y = mm(lhs[...], jnp.concatenate([hi, lo], axis=0))
        return y[:side] + y[side:]

    def uncolumn(y):
        return jnp.concatenate(
            [y[:, :LANES].reshape(SIDE, HALF, LANES), y[:, LANES:].reshape(SIDE, HALF, LANES)], axis=1
        )

    def phase_b(j, carry):
        r = along_i(lhs_f, column_pair(z_ref, j))
        x = column_pair(x_ref, j).astype(BF16)
        k = mm(lhs_k[...], jnp.concatenate([x, x], axis=0))
        v = along_i(lhs_ft, r * column_pair(pot_ref, j))
        v_ref[:, j] = uncolumn(v)
        kin_ref[:, j] += uncolumn(k)
        hi, lo = split2(diag2 * r * r)
        d = mm(
            jnp.concatenate(
                [
                    jnp.concatenate([hi[:, :LANES], lo[:, :LANES]], axis=1),
                    jnp.concatenate([hi[:, LANES:], lo[:, LANES:]], axis=1),
                ],
                axis=0,
            ),
            ones,
        )
        d = d.reshape(2, SIDE, HALF, LANES)
        base = jnp.bitwise_and(j, HALF - 1) * SIDE
        total = acc_ref[jnp.right_shift(j, 3)]
        for h in (0, 1):
            here = lane == sub + (base + h * HALF)
            total = total + jnp.where(here[None], d[h], 0.0)
        acc_ref[jnp.right_shift(j, 3)] = total
        return carry

    lax.fori_loop(0, SIDE, phase_b, 0, unroll=2)

    def gradient(p):
        g = mm(lhs_b[...], stack3(planes(v_ref, p))) + planes(kin_ref, p)
        grad_ref[p] = g.astype(BF16)

    def dispatch(p):
        for h in (0, 1):
            sent = lax.dot_general(
                sel_ref[...], grad_ref[p, :, h * LANES : (h + 1) * LANES], NT, preferred_element_type=F32
            )
            for c in (0, 1):
                rows_ref[:, 4 * p + 2 * h + c] = sent[:, c * LANES : (c + 1) * LANES].reshape(
                    CAP * groups // 8, 8, LANES
                )

    gradient(0)
    for p in range(1, SIDE // 2):
        gradient(p)
        dispatch(p - 1)
    dispatch(SIDE // 2 - 1)
    dens_ref[...] = jnp.concatenate([jnp.sum(acc_ref[0], axis=1), jnp.sum(acc_ref[1], axis=1)], axis=1)

    flat = rows_ref.reshape(CAP * groups * CHUNKS, LANES)
    bands = 4
    per = groups // bands

    def pack(g, carry):
        tile, within = jnp.right_shift(g, 3), jnp.bitwise_and(g, 7)
        for s in range(CAP):
            row = (s * (groups // 8) + tile) * (8 * CHUNKS) + within
            stage_ref[g, s * CHUNKS : (s + 1) * CHUNKS, :] = flat[pl.ds(row, CHUNKS, stride=8), :].astype(BF16)
        return carry

    outs = []
    for b in range(bands):
        lax.fori_loop(b * per, (b + 1) * per, pack, 0, unroll=8)
        part = pl.ds(b * per, per)
        outs.append(pltpu.make_async_copy(stage_ref.at[part], out_hbm.at[part], sem_o.at[b]))
        outs[-1].start()
    for c in outs:
        c.wait()


def run_apply(support, potential, magic_taps, kinetic_taps, kernel_diag, owners, groups):
    box = pltpu.VMEM((SIDE, SIDE, SIDE, LANES), F32)
    side = SIDE * HALF
    side_lhs = pltpu.VMEM((2 * side, 2 * side), BF16)
    dma = pltpu.SemaphoreType.DMA((4,))
    return pl.pallas_call(
        functools.partial(apply_kernel, groups),
        out_shape=(
            jax.ShapeDtypeStruct((groups, BLOCK, LANES), BF16),
            jax.ShapeDtypeStruct((SIDE, PLANE), F32),
        ),
        in_specs=[HBM] * 6,
        out_specs=(HBM, VM),
        scratch_shapes=[
            box, box, box, box, box,
            pltpu.VMEM((3, SIDE, PLANE), F32),
            pltpu.VMEM((2 * PLANE, 2 * PLANE), BF16),
            pltpu.VMEM((PLANE, 3 * PLANE), BF16),
            side_lhs, side_lhs,
            pltpu.VMEM((side, 2 * side), BF16),
            pltpu.VMEM((CAP * groups, LANES), BF16),
            pltpu.VMEM((CAP * groups // 8, CHUNKS, 8, LANES), F32),
            pltpu.VMEM((2, SIDE, HALF, LANES), F32),
            pltpu.VMEM((groups, BLOCK, LANES), BF16),
            pltpu.VMEM((SIDE // 2, PLANE, 2 * LANES), BF16),
            pltpu.SMEM((SIDE,), F32), pltpu.SMEM((SIDE,), F32),
            pltpu.VMEM((1, LANES), F32), pltpu.VMEM((1, LANES), jnp.int32),
            dma, dma, dma, dma,
        ],
        compiler_params=pltpu.CompilerParams(vmem_limit_bytes=67043328),
        name="apply",
    )(magic_taps, kinetic_taps, kernel_diag.reshape(1, LANES), owners.reshape(1, LANES), support, potential)


def select_kernel(groups, owner_ref, out_ref):
    owner = owner_ref[...]
    column = slot_of(owner) * groups + owner
    down = jnp.broadcast_to(column.astype(F32), (LANES, LANES)).T
    lane = lax.broadcasted_iota(jnp.int32, (LANES, LANES), 1).astype(F32)
    for t in range(CAP * groups // LANES + 1):
        out_ref[:, t * LANES : (t + 1) * LANES] = jnp.where(down == lane + float(t * LANES), 1.0, 0.0).astype(BF16)


def run_select(owners, groups):
    return pl.pallas_call(
        functools.partial(select_kernel, groups),
        out_shape=jax.ShapeDtypeStruct((LANES, 2 * LANES), BF16),
        in_specs=[VM],
        out_specs=VM,
        name="select",
    )(owners.reshape(1, LANES))


def margin_kernel(groups, recv_hbm, coef_ref, scale_ref, slab_ref, out_ref, recv_ref, rows_ref, sem):
    bands = 4
    per = groups // bands
    copies = []
    for b in range(bands):
        part = pl.ds(b * per, per)
        copies.append(pltpu.make_async_copy(recv_hbm.at[part], recv_ref.at[part], sem.at[b]))
        copies[-1].start()
    flat = rows_ref.reshape(CAP * groups * CHUNKS, LANES)

    def unpack(g, carry):
        tile, within = jnp.right_shift(g, 3), jnp.bitwise_and(g, 7)
        for s in range(CAP):
            row = (s * (groups // 8) + tile) * (8 * CHUNKS) + within
            flat[pl.ds(row, CHUNKS, stride=8), :] = recv_ref[g, s * CHUNKS : (s + 1) * CHUNKS, :].astype(F32)
        return carry

    for b in range(bands):
        copies[b].wait()
        lax.fori_loop(b * per, (b + 1) * per, unpack, 0, unroll=4)

    def step(i, acc):
        cols = [rows_ref[:, 2 * i + c].reshape(CAP * groups, LANES) for c in (0, 1)]
        lhs = jnp.concatenate(cols, axis=1).astype(BF16)
        return acc + mm(lhs, coef_ref[pl.ds(pl.multiple_of(i * PLANE, PLANE), PLANE), :])

    acc = lax.fori_loop(0, SIDE, step, jnp.zeros((CAP * groups, LANES), F32), unroll=4)
    acc = acc * (scale_ref[...] * (1.0 / float(SIDE) ** 1.5))
    for s in range(CAP):
        out_ref[pl.ds(s, groups, stride=BACK), :] = acc[s * groups : (s + 1) * groups]
    slab = slab_ref[...]
    for h in range(2):
        out_ref[pl.ds(CAP + h, groups, stride=BACK), :] = jnp.broadcast_to(
            slab[:, h * LANES : (h + 1) * LANES], (groups, LANES)
        )
    for s in range(CAP + 2, BACK):
        out_ref[pl.ds(s, groups, stride=BACK), :] = jnp.zeros((groups, LANES), F32)


def run_margin(received, owned, kernel_diag, slab, groups):
    return pl.pallas_call(
        functools.partial(margin_kernel, groups),
        out_shape=jax.ShapeDtypeStruct((groups * BACK, LANES), F32),
        in_specs=[HBM, VM, VM, VM],
        out_specs=VM,
        scratch_shapes=[
            pltpu.VMEM((groups, BLOCK, LANES), BF16),
            pltpu.VMEM((CAP * groups // 8, CHUNKS, 8, LANES), F32),
            pltpu.SemaphoreType.DMA((4,)),
        ],
        compiler_params=pltpu.CompilerParams(vmem_limit_bytes=16 * 1024 * 1024),
        name="margin",
    )(received, owned, kernel_diag.reshape(1, LANES), slab)


def gather_kernel(groups, select_ref, ret_ref, out_ref, dens_ref):
    rows = [ret_ref[pl.ds(s, groups, stride=BACK), :] for s in range(CAP + 2)]
    x = jnp.concatenate(rows[:CAP] + [jnp.zeros((groups, LANES), F32)], axis=0)
    hi, mid = split2(x)
    lo = (x - hi.astype(F32) - mid.astype(F32)).astype(BF16)
    y = mm(select_ref[...], jnp.concatenate([hi, mid], axis=1))
    out_ref[...] = y[:, :LANES] + (y[:, LANES:] + mm(select_ref[...], lo))
    for h in range(2):
        dens_ref[:, h * LANES : (h + 1) * LANES] = jnp.sum(
            rows[CAP + h].reshape(groups // HALF, HALF, LANES), axis=0
        )


def run_gather(select, returned, groups):
    return pl.pallas_call(
        functools.partial(gather_kernel, groups),
        out_shape=(
            jax.ShapeDtypeStruct((LANES, LANES), F32),
            jax.ShapeDtypeStruct((HALF, PLANE), F32),
        ),
        in_specs=[VM, VM],
        out_specs=(VM, VM),
        name="gather",
    )(select, returned)


def body(support, potential, magic_taps, kinetic_taps, kernel_diag, owners):
    groups = lax.axis_size("grp")
    domains = lax.axis_size("dom")
    outgoing, part = run_apply(support, potential, magic_taps, kinetic_taps, kernel_diag, owners, groups)
    received = lax.all_to_all(outgoing, "grp", split_axis=0, concat_axis=0, tiled=True)
    owners_late, support_late, part = lax.optimization_barrier((owners, support, part))
    select = run_select(owners_late, groups)
    owned = support_late.reshape(CELLS, LANES).astype(BF16)
    distance = 1
    while distance < HALF:
        part = part + lax.ppermute(part, "grp", [(i, i ^ distance) for i in range(groups)])
        distance *= 2
    upper = lax.ppermute(part[HALF:], "dom", [(i, (i + 1) % domains) for i in range(domains)])
    mine = lax.axis_index("grp") % HALF
    slab = lax.dynamic_slice_in_dim(part[:HALF] + upper, mine, 1, 0)
    products = run_margin(received, owned, kernel_diag, slab, groups)
    returned = lax.all_to_all(
        products.reshape(groups, BACK, LANES), "grp", split_axis=0, concat_axis=0, tiled=True
    )
    return run_gather(select, returned.reshape(groups * BACK, LANES), groups)


def solution(mesh):
    return jax.shard_map(
        body,
        mesh=mesh,
        in_specs=(
            P(None, None, None, ("dom", "grp")),
            P(None, None, None, ("dom", "grp")),
            P(),
            P(),
            P(("dom", "grp")),
            P(("dom", "grp"), None),
        ),
        out_specs=(P(("dom", "grp"), None), P("dom", None)),
        check_vma=False,
    )
```

time: 121 us -> 94.6 us (0.78)
  starting transfers between devices: 49.6 us -> 33.6 us
  local copies, waits for them, and re-layouts: 7.58 us -> 0.72 us
  Pallas kernels: 26.1 us -> 20.8 us
  waiting for transfers between devices: 35.1 us -> 36.4 us
    ppermute x6 -> x3, waiting for transfers between devices: 24.6 us -> 4.03 us  [body(): lax.ppermute(part, 'grp', [(i, i ^ distance) for i in range(groups)])]
    ppermute x6 -> x3, starting transfers between devices: 22.9 us -> 10.6 us  [body(): lax.ppermute(part, 'grp', [(i, i ^ distance) for i in range(groups)])]
    all_to_all x1, waiting for transfers between devices: 0.01 us -> 11.7 us  [body(): lax.all_to_all(products.reshape(groups, BACK, LANES), 'grp', split_axis=0...]
    all_to_all x1, waiting for transfers between devices: 0.87 us -> 11.9 us  [body(): lax.all_to_all(outgoing, 'grp', split_axis=0, concat_axis=0, tiled=True)]
    unnamed x20 -> x6, local copies, waits for them, and re-layouts: 7.57 us -> 0.72 us
    pallas_call x1, Pallas kernels: 18.2 us -> 14.2 us  [run_apply(): pl.pallas_call(functools.partial(apply_kernel, groups), out_shape=(jax.Sh...]
    all_to_all x1, starting transfers between devices: 9.21 us -> 6.47 us  [body(): lax.all_to_all(products.reshape(groups, BACK, LANES), 'grp', split_axis=0...]
    pallas_call x1, Pallas kernels: 6.05 us -> 3.31 us  [run_margin(): pl.pallas_call(functools.partial(margin_kernel, groups), out_shape=jax.Sh...]
  transfers between devices with their start and end apart: 9 -> 6, of which waited for: 7 -> 6; matrix products, arithmetic and copies ran while one was open for 1% -> 2% of each run, Pallas kernels for 5% -> 2%
where the time goes in v2:
time: 94.6 us; the launch traced here: 94.1 us
  waiting for transfers between devices  36.4 us (38%)
  starting transfers between devices  33.6 us (36%)
  Pallas kernels  20.8 us (22%)
  other arithmetic  1.77 us (2%)
    all_to_all x1, starting transfers between devices, body(): lax.all_to_all(outgoing, 'grp', split_axis=0, concat_axis=0, tiled=True)  14.6 us
    pallas_call x1, Pallas kernels, run_apply(): pl.pallas_call(functools.partial(apply_kernel, groups), out_shape=(jax.Sh...  14.2 us
    all_to_all x1, waiting for transfers between devices, body(): lax.all_to_all(outgoing, 'grp', split_axis=0, concat_axis=0, tiled=True)  11.9 us
    all_to_all x1, waiting for transfers between devices, body(): lax.all_to_all(products.reshape(groups, BACK, LANES), 'grp', split_axis=0...  11.7 us
    ppermute x3, starting transfers between devices, body(): lax.ppermute(part, 'grp', [(i, i ^ distance) for i in range(groups)])  10.6 us
    ppermute x1, waiting for transfers between devices, body(): lax.ppermute(part[HALF:], 'dom', [(i, (i + 1) % domains) for i in range(d...  8.77 us
    all_to_all x1, starting transfers between devices, body(): lax.all_to_all(products.reshape(groups, BACK, LANES), 'grp', split_axis=0...  6.47 us
    ppermute x3, waiting for transfers between devices, body(): lax.ppermute(part, 'grp', [(i, i ^ distance) for i in range(groups)])  4.03 us
  transfers between devices with their start and end apart: 6, of which 6 were waited for; matrix products, arithmetic and copies ran while one was open for 2% of the time, Pallas kernels for 2%

profile of v2, /device:TPU:1, one launch (start us, length us, event | category | flops | bytes accessed | tf_op | source)
XLA Modules:
  0.0 94.1 jit_solution(6232175960231079684)
XLA Ops:
  0.6 14.2 %apply.1 = (bf16[64,96,128]{2,1,0:T(8,128)(2,1)}, f32[16,256]{1,0:T(8,128)}) custom-call(f32[16]{0:T(128)} %magic_hbm.1, f32[16]{0:T(128)} %kinetic_hbm.1, f32[1,128]{1,0:T(1,128)} %bitcast.7, s32[1,128]{1,0:T(1,128)} %bitcast.10, f32[16,16,16,128]{3,2,1,0:T(8,128)} %x_hbm.1, f32[16,16,16,128]{3,2,1,0:T(8,128)} %pot_hbm.1), custom_call_target="tpu_custom_call" | custom-call | tf_op jit(solution)/shard_map/apply/pallas_call | solution.py:267
  14.9 0.0 copy-start.2
  14.9 14.6 %all-to-all-start = ((bf16[64,96,128]{2,1,0:T(8,128)(2,1)}), bf16[64,96,128]{2,1,0:T(8,128)(2,1)S(1)}, u32[]{:S(2)}, u32[]{:S(2)}) async-start(bf16[64,96,128]{2,1,0:T(8,128)(2,1)} %get-tuple-element.9), calls=%async_computation | async-start | bytes 3145728 | tf_op jit(solution)/shard_map/all_to_all | solution.py:400
  29.5 0.0 copy-start
  29.5 0.0 copy-done.2
  29.5 2.5 %collective-permute-start = (f32[16,256]{1,0:T(8,128)S(1)}, f32[16,256]{1,0:T(8,128)S(1)}, u32[]{:S(2)}, u32[]{:S(2)}) collective-permute-start(f32[16,256]{1,0:T(8,128)S(1)} %copy-done.2), channel_id=1, source_target_pairs={{0,1},{1,0},{2,3},{3,2},{4,5},{5,4},{6,7},{7,6},{8,9},{9,8},{10,11... | collective-permute-start | bytes 49160 | tf_op jit(solution)/shard_map/ppermute | solution.py:406
  32.0 0.8 collective-permute-done
  32.8 3.1 %collective-permute-start.1 = (f32[16,256]{1,0:T(8,128)S(1)}, f32[16,256]{1,0:T(8,128)S(1)}, u32[]{:S(2)}, u32[]{:S(2)}) collective-permute-start(f32[16,256]{1,0:T(8,128)S(1)} %add.19), channel_id=1, source_target_pairs={{0,2},{1,3},{2,0},{3,1},{4,6},{5,7},{6,4},{7,5},{8,10},{9,11},{10,... | collective-permute-start | bytes 49160 | tf_op jit(solution)/shard_map/ppermute | solution.py:406
  35.9 1.8 %collective-permute-done.1 = f32[16,256]{1,0:T(8,128)S(1)} collective-permute-done((f32[16,256]{1,0:T(8,128)S(1)}, f32[16,256]{1,0:T(8,128)S(1)}, u32[]{:S(2)}, u32[]{:S(2)}) %collective-permute-start.1) | collective-permute-done | bytes 16416 | tf_op jit(solution)/shard_map/ppermute | solution.py:406
  37.7 5.1 %collective-permute-start.2 = (f32[16,256]{1,0:T(8,128)S(1)}, f32[16,256]{1,0:T(8,128)S(1)}, u32[]{:S(2)}, u32[]{:S(2)}) collective-permute-start(f32[16,256]{1,0:T(8,128)S(1)} %add.20), channel_id=1, source_target_pairs={{0,4},{1,5},{2,6},{3,7},{4,0},{5,1},{6,2},{7,3},{8,12},{9,13},{10,... | collective-permute-start | bytes 49160 | tf_op jit(solution)/shard_map/ppermute | solution.py:406
  42.8 1.5 %collective-permute-done.2 = f32[16,256]{1,0:T(8,128)S(1)} collective-permute-done((f32[16,256]{1,0:T(8,128)S(1)}, f32[16,256]{1,0:T(8,128)S(1)}, u32[]{:S(2)}, u32[]{:S(2)}) %collective-permute-start.2) | collective-permute-done | bytes 16416 | tf_op jit(solution)/shard_map/ppermute | solution.py:406
  44.2 1.9 %collective-permute-start.3 = (f32[8,256]{1,0:T(8,128)S(1)}, f32[8,256]{1,0:T(8,128)S(1)}, u32[]{:S(2)}, u32[]{:S(2)}) collective-permute-start(f32[8,256]{1,0:T(8,128)S(1)} %get-tuple-element.13), channel_id=1, source_target_pairs={{0,64},{64,128},{128,192},{192,256},{256,320},{320,384},{384,448},... | collective-permute-start | bytes 24584 | tf_op jit(solution)/shard_map/ppermute | solution.py:408
  46.2 1.8 %convert_element_type.5 = bf16[16,16,16,128]{3,2,1,0:T(8,128)(2,1)S(1)} convert(f32[16,16,16,128]{3,2,1,0:T(8,128)} %x_hbm.1) | non-fusion elementwise | flops 524288 | bytes 3145728 | tf_op jit(solution)/shard_map/convert_element_type | solution.py:403
  47.9 8.8 %collective-permute-done.3 = f32[8,256]{1,0:T(8,128)S(1)} collective-permute-done((f32[8,256]{1,0:T(8,128)S(1)}, f32[8,256]{1,0:T(8,128)S(1)}, u32[]{:S(2)}, u32[]{:S(2)}) %collective-permute-start.3) | collective-permute-done | bytes 8224 | tf_op jit(solution)/shard_map/ppermute | solution.py:408
  56.7 11.9 %all-to-all-done.recv_hbm = bf16[64,96,128]{2,1,0:T(8,128)(2,1)S(1)} async-done(((bf16[64,96,128]{2,1,0:T(8,128)(2,1)}), bf16[64,96,128]{2,1,0:T(8,128)(2,1)S(1)}, u32[]{:S(2)}, u32[]{:S(2)}) %all-to-all-start) | async-done | bytes 1572896 | tf_op jit(solution)/shard_map/all_to_all | solution.py:400
  68.6 0.0 copy-done
  68.6 3.3 %margin.1 = f32[512,128]{1,0:T(8,128)} custom-call(bf16[64,96,128]{2,1,0:T(8,128)(2,1)S(1)} %all-to-all-done.recv_hbm, bf16[4096,128]{1,0:T(8,128)(2,1)S(1)} %bitcast.6, f32[1,128]{1,0:T(1,128)S(1)} %bitcast.8, f32[1,256]{1,0:T(1,128)S(1)} %dynamic-slice_add_fusion.slab_ref), custom_call_target="tpu_custom_call" | custom-call | tf_op jit(solution)/shard_map/margin/pallas_call | solution.py:355
  72.0 6.5 %all-to-all-start.1 = ((f32[64,8,128]{2,1,0:T(8,128)}), f32[64,8,128]{2,1,0:T(8,128)S(1)}, u32[]{:S(2)}, u32[]{:S(2)}) async-start(f32[64,8,128]{2,1,0:T(8,128)} %bitcast.4), calls=%async_computation.1 | async-start | bytes 524288 | tf_op jit(solution)/shard_map/all_to_all | solution.py:412
  78.4 1.5 %select.3.select_ref = bf16[128,256]{1,0:T(8,128)(2,1)} custom-call(s32[1,128]{1,0:T(1,128)} %bitcast.11), custom_call_target="tpu_custom_call" | custom-call | tf_op jit(solution)/shard_map/select/pallas_call | solution.py:306
  79.9 11.7 %all-to-all-done.1 = f32[64,8,128]{2,1,0:T(8,128)S(1)} async-done(((f32[64,8,128]{2,1,0:T(8,128)}), f32[64,8,128]{2,1,0:T(8,128)S(1)}, u32[]{:S(2)}, u32[]{:S(2)}) %all-to-all-start.1) | async-done | bytes 262176 | tf_op jit(solution)/shard_map/all_to_all | solution.py:412
  91.6 0.0 copy-start.1
  91.6 0.7 copy-done.1
  92.3 1.8 %gather.1 = (f32[128,128]{1,0:T(8,128)}, f32[8,256]{1,0:T(8,128)}) custom-call(bf16[128,256]{1,0:T(8,128)(2,1)} %select.3.select_ref, f32[512,128]{1,0:T(8,128)} %bitcast.9), custom_call_target="tpu_custom_call" | custom-call | tf_op jit(solution)/shard_map/gather/pallas_call | solution.py:384
  (5 shorter events, 0.0 us)
Async XLA Ops:
  14.9 14.7 %copy-start.2 = (f32[16,256]{1,0:T(8,128)S(1)}, f32[16,256]{1,0:T(8,128)}, u32[]{:S(2)}) copy-start(f32[16,256]{1,0:T(8,128)} %get-tuple-element.11) | copy-start | bytes 49156
  14.9 53.8 %all-to-all-start = ((bf16[64,96,128]{2,1,0:T(8,128)(2,1)}), bf16[64,96,128]{2,1,0:T(8,128)(2,1)S(1)}, u32[]{:S(2)}, u32[]{:S(2)}) async-start(bf16[64,96,128]{2,1,0:T(8,128)(2,1)} %get-tuple-element.9), calls=%async_computation | async-start | bytes 3145728 | tf_op jit(solution)/shard_map/all_to_all | solution.py:400
  29.5 39.1 %copy-start = (f32[128]{0:T(128)S(1)}, f32[128]{0:T(128)}, u32[]{:S(2)}) copy-start(f32[128]{0:T(128)} %param.10) | copy-start | bytes 1540
  29.5 3.3 %collective-permute-start = (f32[16,256]{1,0:T(8,128)S(1)}, f32[16,256]{1,0:T(8,128)S(1)}, u32[]{:S(2)}, u32[]{:S(2)}) collective-permute-start(f32[16,256]{1,0:T(8,128)S(1)} %copy-done.2), channel_id=1, source_target_pairs={{0,1},{1,0},{2,3},{3,2},{4,5},{5,4},{6,7},{7,6},{8,9},{9,8},{10,11... | collective-permute-start | bytes 49160 | tf_op jit(solution)/shard_map/ppermute | solution.py:406
  32.8 4.8 %collective-permute-start.1 = (f32[16,256]{1,0:T(8,128)S(1)}, f32[16,256]{1,0:T(8,128)S(1)}, u32[]{:S(2)}, u32[]{:S(2)}) collective-permute-start(f32[16,256]{1,0:T(8,128)S(1)} %add.19), channel_id=1, source_target_pairs={{0,2},{1,3},{2,0},{3,1},{4,6},{5,7},{6,4},{7,5},{8,10},{9,11},{10,... | collective-permute-start | bytes 49160 | tf_op jit(solution)/shard_map/ppermute | solution.py:406
  37.7 6.5 %collective-permute-start.2 = (f32[16,256]{1,0:T(8,128)S(1)}, f32[16,256]{1,0:T(8,128)S(1)}, u32[]{:S(2)}, u32[]{:S(2)}) collective-permute-start(f32[16,256]{1,0:T(8,128)S(1)} %add.20), channel_id=1, source_target_pairs={{0,4},{1,5},{2,6},{3,7},{4,0},{5,1},{6,2},{7,3},{8,12},{9,13},{10,... | collective-permute-start | bytes 49160 | tf_op jit(solution)/shard_map/ppermute | solution.py:406
  44.2 12.5 %collective-permute-start.3 = (f32[8,256]{1,0:T(8,128)S(1)}, f32[8,256]{1,0:T(8,128)S(1)}, u32[]{:S(2)}, u32[]{:S(2)}) collective-permute-start(f32[8,256]{1,0:T(8,128)S(1)} %get-tuple-element.13), channel_id=1, source_target_pairs={{0,64},{64,128},{128,192},{192,256},{256,320},{320,384},{384,448},... | collective-permute-start | bytes 24584 | tf_op jit(solution)/shard_map/ppermute | solution.py:408
  72.0 19.6 %all-to-all-start.1 = ((f32[64,8,128]{2,1,0:T(8,128)}), f32[64,8,128]{2,1,0:T(8,128)S(1)}, u32[]{:S(2)}, u32[]{:S(2)}) async-start(f32[64,8,128]{2,1,0:T(8,128)} %bitcast.4), calls=%async_computation.1 | async-start | bytes 524288 | tf_op jit(solution)/shard_map/all_to_all | solution.py:412
  91.6 0.7 copy-start.1

commit v3 on v2

--- a/solution.py
+++ b/solution.py
@@ -113,8 +113,8 @@
     groups,
     magic_hbm, kinetic_hbm, diag_hbm, owner_hbm, x_hbm, pot_hbm,
     out_hbm, dens_ref,
-    x_ref, pot_ref, z_ref, kin_ref, v_ref,
-    pat_ref, lhs1, lhs_b, lhs_f, lhs_ft, lhs_k, sel_ref, rows_ref, acc_ref, stage_ref, grad_ref,
+    x_ref, pot_ref, z_ref, kin_ref, kin_i_ref, r_ref, v_ref,
+    pat_ref, lhs1, lhs_b, lhs_f, lhs_ft, lhs_k, sel_ref, rows_ref, stage_ref, grad_ref,
     magic, kinetic, diag_ref, owner_ref,
     sem_s, sem_x, sem_p, sem_o,
 ):
@@ -144,7 +144,6 @@
     column = slot_of(owner) * groups + owner
     ri = lax.broadcasted_iota(jnp.int32, (CAP * groups, LANES), 0)
     sel_ref[...] = jnp.where(ri == column, 1.0, 0.0).astype(BF16)
-    acc_ref[...] = jnp.zeros_like(acc_ref)
 
     def planes(ref, p):
         a, b = ref[2 * p], ref[2 * p + 1]
@@ -159,16 +158,15 @@
             kin_ref[2 * p + h] = y[PLANE:, cols].reshape(SIDE, SIDE, LANES)
         return carry
 
-    for q in range(parts):
-        copies_x[q].wait()
-        lax.fori_loop(q * width // 2, (q + 1) * width // 2, phase_a, 0, unroll=True)
+    for c in copies_x:
+        c.wait()
+    lax.fori_loop(0, SIDE // 2, phase_a, 0, unroll=4)
     for c in copies_p:
         c.wait()
 
     side = SIDE * HALF
     diag = diag_ref[...] * (1.0 / (LANES * groups))
     diag2 = jnp.concatenate([diag, diag], axis=1)
-    ones = jnp.ones((2 * LANES, LANES), BF16)
     lane = lax.broadcasted_iota(jnp.int32, (HALF, LANES), 1)
     sub = lax.broadcasted_iota(jnp.int32, (HALF, LANES), 0)
 
@@ -183,42 +181,43 @@
         y = mm(lhs[...], jnp.concatenate([hi, lo], axis=0))
         return y[:side] + y[side:]
 
-    def uncolumn(y):
-        return jnp.concatenate(
-            [y[:, :LANES].reshape(SIDE, HALF, LANES), y[:, LANES:].reshape(SIDE, HALF, LANES)], axis=1
-        )
-
-    def phase_b(j, carry):
-        r = along_i(lhs_f, column_pair(z_ref, j))
+    def filter_out(j):
+        r_ref[j] = along_i(lhs_f, column_pair(z_ref, j))
         x = column_pair(x_ref, j).astype(BF16)
-        k = mm(lhs_k[...], jnp.concatenate([x, x], axis=0))
-        v = along_i(lhs_ft, r * column_pair(pot_ref, j))
-        v_ref[:, j] = uncolumn(v)
-        kin_ref[:, j] += uncolumn(k)
-        hi, lo = split2(diag2 * r * r)
-        d = mm(
-            jnp.concatenate(
-                [
-                    jnp.concatenate([hi[:, :LANES], lo[:, :LANES]], axis=1),
-                    jnp.concatenate([hi[:, LANES:], lo[:, LANES:]], axis=1),
-                ],
-                axis=0,
-            ),
-            ones,
-        )
-        d = d.reshape(2, SIDE, HALF, LANES)
-        base = jnp.bitwise_and(j, HALF - 1) * SIDE
-        total = acc_ref[jnp.right_shift(j, 3)]
+        kin_i_ref[j] = mm(lhs_k[...], jnp.concatenate([x, x], axis=0))
+
+    def filter_back(j, total):
+        r = r_ref[j]
+        v_ref[j] = along_i(lhs_ft, r * column_pair(pot_ref, j))
+        weighted = diag2 * r * r
         for h in (0, 1):
-            here = lane == sub + (base + h * HALF)
-            total = total + jnp.where(here[None], d[h], 0.0)
-        acc_ref[jnp.right_shift(j, 3)] = total
-        return carry
-
-    lax.fori_loop(0, SIDE, phase_b, 0, unroll=2)
+            here = lane == sub + (jnp.bitwise_and(j, HALF - 1) * SIDE + h * HALF)
+            d = jnp.sum(weighted[:, h * LANES : (h + 1) * LANES], axis=1, keepdims=True)
+            d = jnp.broadcast_to(d, (side, LANES)).reshape(SIDE, HALF, LANES)
+            total = total + jnp.where(here[None], d, 0.0)
+        return total
+
+    filter_out(0)
+    total = jnp.zeros((SIDE, HALF, LANES), F32)
+    for j in range(SIDE):
+        if j + 1 < SIDE:
+            filter_out(j + 1)
+        total = filter_back(j, total)
+        if j % HALF == HALF - 1:
+            t = j // HALF
+            dens_ref[:, t * LANES : (t + 1) * LANES] = jnp.sum(total, axis=1)
+            total = jnp.zeros((SIDE, HALF, LANES), F32)
+
+    def slab_planes(ref, p):
+        def one(i):
+            rows = pl.ds(i * HALF, HALF)
+            both = [ref[:, rows, h * LANES : (h + 1) * LANES] for h in (0, 1)]
+            return jnp.concatenate(both, axis=1).reshape(PLANE, LANES)
+
+        return jnp.concatenate([one(2 * p), one(2 * p + 1)], axis=1)
 
     def gradient(p):
-        g = mm(lhs_b[...], stack3(planes(v_ref, p))) + planes(kin_ref, p)
+        g = mm(lhs_b[...], stack3(slab_planes(v_ref, p))) + (planes(kin_ref, p) + slab_planes(kin_i_ref, p))
         grad_ref[p] = g.astype(BF16)
 
     def dispatch(p):
@@ -227,31 +226,36 @@
                 sel_ref[...], grad_ref[p, :, h * LANES : (h + 1) * LANES], NT, preferred_element_type=F32
             )
             for c in (0, 1):
-                rows_ref[:, 4 * p + 2 * h + c] = sent[:, c * LANES : (c + 1) * LANES].reshape(
-                    CAP * groups // 8, 8, LANES
-                )
+                chunk = 4 * p + 2 * h + c
+                place = chunk // 8 * 64 + chunk % 8
+                for t in range(CAP * groups // 8):
+                    rows_ref[pl.ds(place + t * 8 * CHUNKS, 8, stride=8), :] = sent[
+                        t * 8 : t * 8 + 8, c * LANES : (c + 1) * LANES
+                    ]
+
+    def stage(p, carry):
+        gradient(p)
+        dispatch(p - 1)
+        return carry
 
     gradient(0)
     for p in range(1, SIDE // 2):
-        gradient(p)
-        dispatch(p - 1)
+        stage(p, 0)
     dispatch(SIDE // 2 - 1)
-    dens_ref[...] = jnp.concatenate([jnp.sum(acc_ref[0], axis=1), jnp.sum(acc_ref[1], axis=1)], axis=1)
-
-    flat = rows_ref.reshape(CAP * groups * CHUNKS, LANES)
     bands = 4
     per = groups // bands
 
-    def pack(g, carry):
-        tile, within = jnp.right_shift(g, 3), jnp.bitwise_and(g, 7)
+    def pack(g):
+        tile, within = g // 8, g % 8
         for s in range(CAP):
-            row = (s * (groups // 8) + tile) * (8 * CHUNKS) + within
-            stage_ref[g, s * CHUNKS : (s + 1) * CHUNKS, :] = flat[pl.ds(row, CHUNKS, stride=8), :].astype(BF16)
-        return carry
+            row = (s * (groups // 8) + tile) * (8 * CHUNKS) + within * 8
+            parts = [rows_ref[pl.ds(row + q * 64, 8), :] for q in range(CHUNKS // 8)]
+            stage_ref[g, s * CHUNKS : (s + 1) * CHUNKS, :] = jnp.concatenate(parts, axis=0).astype(BF16)
 
     outs = []
     for b in range(bands):
-        lax.fori_loop(b * per, (b + 1) * per, pack, 0, unroll=8)
+        for g in range(b * per, (b + 1) * per):
+            pack(g)
         part = pl.ds(b * per, per)
         outs.append(pltpu.make_async_copy(stage_ref.at[part], out_hbm.at[part], sem_o.at[b]))
         outs[-1].start()
@@ -262,6 +266,7 @@
 def run_apply(support, potential, magic_taps, kinetic_taps, kernel_diag, owners, groups):
     box = pltpu.VMEM((SIDE, SIDE, SIDE, LANES), F32)
     side = SIDE * HALF
+    slab = pltpu.VMEM((SIDE, side, 2 * LANES), F32)
     side_lhs = pltpu.VMEM((2 * side, 2 * side), BF16)
     dma = pltpu.SemaphoreType.DMA((4,))
     return pl.pallas_call(
@@ -273,15 +278,14 @@
         in_specs=[HBM] * 6,
         out_specs=(HBM, VM),
         scratch_shapes=[
-            box, box, box, box, box,
+            box, box, box, box, slab, slab, slab,
             pltpu.VMEM((3, SIDE, PLANE), F32),
             pltpu.VMEM((2 * PLANE, 2 * PLANE), BF16),
             pltpu.VMEM((PLANE, 3 * PLANE), BF16),
             side_lhs, side_lhs,
             pltpu.VMEM((side, 2 * side), BF16),
             pltpu.VMEM((CAP * groups, LANES), BF16),
-            pltpu.VMEM((CAP * groups // 8, CHUNKS, 8, LANES), F32),
-            pltpu.VMEM((2, SIDE, HALF, LANES), F32),
+            pltpu.VMEM((CAP * groups * CHUNKS, LANES), F32),
             pltpu.VMEM((groups, BLOCK, LANES), BF16),
             pltpu.VMEM((SIDE // 2, PLANE, 2 * LANES), BF16),
             pltpu.SMEM((SIDE,), F32), pltpu.SMEM((SIDE,), F32),
@@ -312,33 +316,25 @@
     )(owners.reshape(1, LANES))
 
 
-def margin_kernel(groups, recv_hbm, coef_ref, scale_ref, slab_ref, out_ref, recv_ref, rows_ref, sem):
-    bands = 4
-    per = groups // bands
-    copies = []
-    for b in range(bands):
-        part = pl.ds(b * per, per)
-        copies.append(pltpu.make_async_copy(recv_hbm.at[part], recv_ref.at[part], sem.at[b]))
-        copies[-1].start()
-    flat = rows_ref.reshape(CAP * groups * CHUNKS, LANES)
-
-    def unpack(g, carry):
-        tile, within = jnp.right_shift(g, 3), jnp.bitwise_and(g, 7)
+def margin_kernel(groups, recv_ref, coef_ref, scale_ref, slab_ref, out_ref, rows_ref):
+    for g in range(groups):
         for s in range(CAP):
-            row = (s * (groups // 8) + tile) * (8 * CHUNKS) + within
-            flat[pl.ds(row, CHUNKS, stride=8), :] = recv_ref[g, s * CHUNKS : (s + 1) * CHUNKS, :].astype(F32)
-        return carry
-
-    for b in range(bands):
-        copies[b].wait()
-        lax.fori_loop(b * per, (b + 1) * per, unpack, 0, unroll=4)
-
-    def step(i, acc):
-        cols = [rows_ref[:, 2 * i + c].reshape(CAP * groups, LANES) for c in (0, 1)]
-        lhs = jnp.concatenate(cols, axis=1).astype(BF16)
-        return acc + mm(lhs, coef_ref[pl.ds(pl.multiple_of(i * PLANE, PLANE), PLANE), :])
-
-    acc = lax.fori_loop(0, SIDE, step, jnp.zeros((CAP * groups, LANES), F32), unroll=4)
+            block = recv_ref[g, s * CHUNKS : (s + 1) * CHUNKS, :].astype(F32)
+            row = (s * (groups // 8) + g // 8) * (8 * CHUNKS) + g % 8 * 8
+            for q in range(CHUNKS // 8):
+                rows_ref[pl.ds(row + q * 64, 8), :] = block[q * 8 : q * 8 + 8]
+
+    def column(c):
+        start = c // 8 * 64 + c % 8
+        tiles = [
+            rows_ref[pl.ds(start + t * 8 * CHUNKS, 8, stride=8), :] for t in range(CAP * groups // 8)
+        ]
+        return jnp.concatenate(tiles, axis=0)
+
+    acc = jnp.zeros((CAP * groups, LANES), F32)
+    for i in range(SIDE):
+        lhs = jnp.concatenate([column(2 * i), column(2 * i + 1)], axis=1).astype(BF16)
+        acc = acc + mm(lhs, coef_ref[i * PLANE : (i + 1) * PLANE, :])
     acc = acc * (scale_ref[...] * (1.0 / float(SIDE) ** 1.5))
     for s in range(CAP):
         out_ref[pl.ds(s, groups, stride=BACK), :] = acc[s * groups : (s + 1) * groups]
@@ -355,19 +351,18 @@
     return pl.pallas_call(
         functools.partial(margin_kernel, groups),
         out_shape=jax.ShapeDtypeStruct((groups * BACK, LANES), F32),
-        in_specs=[HBM, VM, VM, VM],
+        in_specs=[VM, VM, VM, VM],
         out_specs=VM,
-        scratch_shapes=[
-            pltpu.VMEM((groups, BLOCK, LANES), BF16),
-            pltpu.VMEM((CAP * groups // 8, CHUNKS, 8, LANES), F32),
-            pltpu.SemaphoreType.DMA((4,)),
-        ],
+        scratch_shapes=[pltpu.VMEM((CAP * groups * CHUNKS, LANES), F32)],
         compiler_params=pltpu.CompilerParams(vmem_limit_bytes=16 * 1024 * 1024),
         name="margin",
     )(received, owned, kernel_diag.reshape(1, LANES), slab)
 
 
-def gather_kernel(groups, select_ref, ret_ref, out_ref, dens_ref):
+def gather_kernel(groups, select_ref, ret_hbm, out_ref, dens_ref, ret_ref, sem):
+    copy = pltpu.make_async_copy(ret_hbm, ret_ref, sem)
+    copy.start()
+    copy.wait()
     rows = [ret_ref[pl.ds(s, groups, stride=BACK), :] for s in range(CAP + 2)]
     x = jnp.concatenate(rows[:CAP] + [jnp.zeros((groups, LANES), F32)], axis=0)
     hi, mid = split2(x)
@@ -387,8 +382,13 @@
             jax.ShapeDtypeStruct((LANES, LANES), F32),
             jax.ShapeDtypeStruct((HALF, PLANE), F32),
         ),
-        in_specs=[VM, VM],
+        in_specs=[VM, HBM],
         out_specs=(VM, VM),
+        scratch_shapes=[
+            pltpu.VMEM((groups * BACK, LANES), F32),
+            pltpu.SemaphoreType.DMA,
+        ],
+        compiler_params=pltpu.CompilerParams(vmem_limit_bytes=4 * 1024 * 1024),
         name="gather",
     )(select, returned)
 

time: 94.6 us -> 87.4 us (0.924)
  Pallas kernels: 20.8 us -> 13.6 us
    pallas_call x1, Pallas kernels: 14.2 us -> 9.56 us  [run_apply(): pl.pallas_call(functools.partial(apply_kernel, groups), out_shape=(jax.Sh...]
    pallas_call x1, Pallas kernels: 3.31 us -> 1.63 us  [run_margin(): pl.pallas_call(functools.partial(margin_kernel, groups), out_shape=jax.Sh...]
    pallas_call x1, Pallas kernels: 1.82 us -> 0.86 us  [run_gather(): pl.pallas_call(functools.partial(gather_kernel, groups), out_shape=(jax.S...]
where the time goes in v3:
time: 87.4 us; the launch traced here: 86.9 us
  waiting for transfers between devices  36.4 us (42%)
  starting transfers between devices  33.6 us (38%)
  Pallas kernels  13.6 us (16%)
  other arithmetic  1.77 us (2%)
    all_to_all x1, starting transfers between devices, body(): lax.all_to_all(outgoing, 'grp', split_axis=0, concat_axis=0, tiled=True)  14.6 us
    all_to_all x1, waiting for transfers between devices, body(): lax.all_to_all(outgoing, 'grp', split_axis=0, concat_axis=0, tiled=True)  11.9 us
    all_to_all x1, waiting for transfers between devices, body(): lax.all_to_all(products.reshape(groups, BACK, LANES), 'grp', split_axis=0...  11.7 us
    ppermute x3, starting transfers between devices, body(): lax.ppermute(part, 'grp', [(i, i ^ distance) for i in range(groups)])  10.6 us
    pallas_call x1, Pallas kernels, run_apply(): pl.pallas_call(functools.partial(apply_kernel, groups), out_shape=(jax.Sh...  9.56 us
    ppermute x1, waiting for transfers between devices, body(): lax.ppermute(part[HALF:], 'dom', [(i, (i + 1) % domains) for i in range(d...  8.77 us
    all_to_all x1, starting transfers between devices, body(): lax.all_to_all(products.reshape(groups, BACK, LANES), 'grp', split_axis=0...  6.45 us
    ppermute x3, waiting for transfers between devices, body(): lax.ppermute(part, 'grp', [(i, i ^ distance) for i in range(groups)])  4.03 us
  transfers between devices with their start and end apart: 6, of which 6 were waited for; matrix products, arithmetic and copies ran while one was open for 2% of the time, Pallas kernels for 2%

profile of v3, /device:TPU:1, one launch (start us, length us, event | category | flops | bytes accessed | tf_op | source)
XLA Modules:
  0.0 86.9 jit_solution(3742560835156133749)
XLA Ops:
  0.6 9.6 %apply.1 = (bf16[64,96,128]{2,1,0:T(8,128)(2,1)}, f32[16,256]{1,0:T(8,128)}) custom-call(f32[16]{0:T(128)} %magic_hbm.1, f32[16]{0:T(128)} %kinetic_hbm.1, f32[1,128]{1,0:T(1,128)} %bitcast.8, s32[1,128]{1,0:T(1,128)} %bitcast.10, f32[16,16,16,128]{3,2,1,0:T(8,128)} %x_hbm.1, f32[16,16,16,128]{3,2,1,0:T(8,128)} %pot_hbm.1), custom_call_target="tpu_custom_call" | custom-call | tf_op jit(solution)/shard_map/apply/pallas_call | solution.py:272
  10.2 0.0 copy-start.2
  10.2 14.6 %all-to-all-start = ((bf16[64,96,128]{2,1,0:T(8,128)(2,1)}), bf16[64,96,128]{2,1,0:T(8,128)(2,1)S(1)}, u32[]{:S(2)}, u32[]{:S(2)}) async-start(bf16[64,96,128]{2,1,0:T(8,128)(2,1)} %get-tuple-element.9), calls=%async_computation | async-start | bytes 3145728 | tf_op jit(solution)/shard_map/all_to_all | solution.py:400
  24.9 0.0 copy-start.1
  24.9 0.0 copy-done.2
  24.9 2.5 %collective-permute-start = (f32[16,256]{1,0:T(8,128)S(1)}, f32[16,256]{1,0:T(8,128)S(1)}, u32[]{:S(2)}, u32[]{:S(2)}) collective-permute-start(f32[16,256]{1,0:T(8,128)S(1)} %copy-done.2), channel_id=1, source_target_pairs={{0,1},{1,0},{2,3},{3,2},{4,5},{5,4},{6,7},{7,6},{8,9},{9,8},{10,11... | collective-permute-start | bytes 49160 | tf_op jit(solution)/shard_map/ppermute | solution.py:406
  27.4 0.8 collective-permute-done
  28.2 3.1 %collective-permute-start.1 = (f32[16,256]{1,0:T(8,128)S(1)}, f32[16,256]{1,0:T(8,128)S(1)}, u32[]{:S(2)}, u32[]{:S(2)}) collective-permute-start(f32[16,256]{1,0:T(8,128)S(1)} %add.19), channel_id=1, source_target_pairs={{0,2},{1,3},{2,0},{3,1},{4,6},{5,7},{6,4},{7,5},{8,10},{9,11},{10,... | collective-permute-start | bytes 49160 | tf_op jit(solution)/shard_map/ppermute | solution.py:406
  31.3 1.8 %collective-permute-done.1 = f32[16,256]{1,0:T(8,128)S(1)} collective-permute-done((f32[16,256]{1,0:T(8,128)S(1)}, f32[16,256]{1,0:T(8,128)S(1)}, u32[]{:S(2)}, u32[]{:S(2)}) %collective-permute-start.1) | collective-permute-done | bytes 16416 | tf_op jit(solution)/shard_map/ppermute | solution.py:406
  33.0 5.1 %collective-permute-start.2 = (f32[16,256]{1,0:T(8,128)S(1)}, f32[16,256]{1,0:T(8,128)S(1)}, u32[]{:S(2)}, u32[]{:S(2)}) collective-permute-start(f32[16,256]{1,0:T(8,128)S(1)} %add.20), channel_id=1, source_target_pairs={{0,4},{1,5},{2,6},{3,7},{4,0},{5,1},{6,2},{7,3},{8,12},{9,13},{10,... | collective-permute-start | bytes 49160 | tf_op jit(solution)/shard_map/ppermute | solution.py:406
  38.1 1.5 %collective-permute-done.2 = f32[16,256]{1,0:T(8,128)S(1)} collective-permute-done((f32[16,256]{1,0:T(8,128)S(1)}, f32[16,256]{1,0:T(8,128)S(1)}, u32[]{:S(2)}, u32[]{:S(2)}) %collective-permute-start.2) | collective-permute-done | bytes 16416 | tf_op jit(solution)/shard_map/ppermute | solution.py:406
  39.6 1.9 %collective-permute-start.3 = (f32[8,256]{1,0:T(8,128)S(1)}, f32[8,256]{1,0:T(8,128)S(1)}, u32[]{:S(2)}, u32[]{:S(2)}) collective-permute-start(f32[8,256]{1,0:T(8,128)S(1)} %get-tuple-element.13), channel_id=1, source_target_pairs={{0,64},{64,128},{128,192},{192,256},{256,320},{320,384},{384,448},... | collective-permute-start | bytes 24584 | tf_op jit(solution)/shard_map/ppermute | solution.py:408
  41.5 1.8 %convert_element_type.5 = bf16[16,16,16,128]{3,2,1,0:T(8,128)(2,1)S(1)} convert(f32[16,16,16,128]{3,2,1,0:T(8,128)} %x_hbm.1) | non-fusion elementwise | flops 524288 | bytes 3145728 | tf_op jit(solution)/shard_map/convert_element_type | solution.py:403
  43.3 8.8 %collective-permute-done.3 = f32[8,256]{1,0:T(8,128)S(1)} collective-permute-done((f32[8,256]{1,0:T(8,128)S(1)}, f32[8,256]{1,0:T(8,128)S(1)}, u32[]{:S(2)}, u32[]{:S(2)}) %collective-permute-start.3) | collective-permute-done | bytes 8224 | tf_op jit(solution)/shard_map/ppermute | solution.py:408
  52.1 11.9 %all-to-all-done.recv_ref = bf16[64,96,128]{2,1,0:T(8,128)(2,1)S(1)} async-done(((bf16[64,96,128]{2,1,0:T(8,128)(2,1)}), bf16[64,96,128]{2,1,0:T(8,128)(2,1)S(1)}, u32[]{:S(2)}, u32[]{:S(2)}) %all-to-all-start) | async-done | bytes 1572896 | tf_op jit(solution)/shard_map/all_to_all | solution.py:400
  64.0 0.0 copy-done.1
  64.0 1.6 %margin.1 = f32[512,128]{1,0:T(8,128)} custom-call(bf16[64,96,128]{2,1,0:T(8,128)(2,1)S(1)} %all-to-all-done.recv_ref, bf16[4096,128]{1,0:T(8,128)(2,1)S(1)} %bitcast.6, f32[1,128]{1,0:T(1,128)S(1)} %bitcast.9, f32[1,256]{1,0:T(1,128)S(1)} %dynamic-slice_add_fusion.slab_ref), custom_call_target="tpu_custom_call" | custom-call | tf_op jit(solution)/shard_map/margin/pallas_call | solution.py:351
  65.6 6.5 %all-to-all-start.1 = ((f32[64,8,128]{2,1,0:T(8,128)}), f32[64,8,128]{2,1,0:T(8,128)S(1)}, u32[]{:S(2)}, u32[]{:S(2)}) async-start(f32[64,8,128]{2,1,0:T(8,128)} %bitcast.4), calls=%async_computation.1 | async-start | bytes 524288 | tf_op jit(solution)/shard_map/all_to_all | solution.py:412
  72.1 1.5 %select.3.select_ref = bf16[128,256]{1,0:T(8,128)(2,1)} custom-call(s32[1,128]{1,0:T(1,128)} %bitcast.11), custom_call_target="tpu_custom_call" | custom-call | tf_op jit(solution)/shard_map/select/pallas_call | solution.py:310
  73.6 11.7 %all-to-all-done.1 = f32[64,8,128]{2,1,0:T(8,128)S(1)} async-done(((f32[64,8,128]{2,1,0:T(8,128)}), f32[64,8,128]{2,1,0:T(8,128)S(1)}, u32[]{:S(2)}, u32[]{:S(2)}) %all-to-all-start.1) | async-done | bytes 262176 | tf_op jit(solution)/shard_map/all_to_all | solution.py:412
  85.2 0.0 copy-start
  85.2 0.8 copy-done
  86.1 0.9 gather.1
  (5 shorter events, 0.0 us)
Async XLA Ops:
  10.2 14.7 %copy-start.2 = (f32[16,256]{1,0:T(8,128)S(1)}, f32[16,256]{1,0:T(8,128)}, u32[]{:S(2)}) copy-start(f32[16,256]{1,0:T(8,128)} %get-tuple-element.11) | copy-start | bytes 49156
  10.2 53.8 %all-to-all-start = ((bf16[64,96,128]{2,1,0:T(8,128)(2,1)}), bf16[64,96,128]{2,1,0:T(8,128)(2,1)S(1)}, u32[]{:S(2)}, u32[]{:S(2)}) async-start(bf16[64,96,128]{2,1,0:T(8,128)(2,1)} %get-tuple-element.9), calls=%async_computation | async-start | bytes 3145728 | tf_op jit(solution)/shard_map/all_to_all | solution.py:400
  24.9 39.1 %copy-start.1 = (f32[128]{0:T(128)S(1)}, f32[128]{0:T(128)}, u32[]{:S(2)}) copy-start(f32[128]{0:T(128)} %param.10) | copy-start | bytes 1540
  24.9 3.3 %collective-permute-start = (f32[16,256]{1,0:T(8,128)S(1)}, f32[16,256]{1,0:T(8,128)S(1)}, u32[]{:S(2)}, u32[]{:S(2)}) collective-permute-start(f32[16,256]{1,0:T(8,128)S(1)} %copy-done.2), channel_id=1, source_target_pairs={{0,1},{1,0},{2,3},{3,2},{4,5},{5,4},{6,7},{7,6},{8,9},{9,8},{10,11... | collective-permute-start | bytes 49160 | tf_op jit(solution)/shard_map/ppermute | solution.py:406
  28.2 4.8 %collective-permute-start.1 = (f32[16,256]{1,0:T(8,128)S(1)}, f32[16,256]{1,0:T(8,128)S(1)}, u32[]{:S(2)}, u32[]{:S(2)}) collective-permute-start(f32[16,256]{1,0:T(8,128)S(1)} %add.19), channel_id=1, source_target_pairs={{0,2},{1,3},{2,0},{3,1},{4,6},{5,7},{6,4},{7,5},{8,10},{9,11},{10,... | collective-permute-start | bytes 49160 | tf_op jit(solution)/shard_map/ppermute | solution.py:406
  33.0 6.5 %collective-permute-start.2 = (f32[16,256]{1,0:T(8,128)S(1)}, f32[16,256]{1,0:T(8,128)S(1)}, u32[]{:S(2)}, u32[]{:S(2)}) collective-permute-start(f32[16,256]{1,0:T(8,128)S(1)} %add.20), channel_id=1, source_target_pairs={{0,4},{1,5},{2,6},{3,7},{4,0},{5,1},{6,2},{7,3},{8,12},{9,13},{10,... | collective-permute-start | bytes 49160 | tf_op jit(solution)/shard_map/ppermute | solution.py:406
  39.6 12.5 %collective-permute-start.3 = (f32[8,256]{1,0:T(8,128)S(1)}, f32[8,256]{1,0:T(8,128)S(1)}, u32[]{:S(2)}, u32[]{:S(2)}) collective-permute-start(f32[8,256]{1,0:T(8,128)S(1)} %get-tuple-element.13), channel_id=1, source_target_pairs={{0,64},{64,128},{128,192},{192,256},{256,320},{320,384},{384,448},... | collective-permute-start | bytes 24584 | tf_op jit(solution)/shard_map/ppermute | solution.py:408
  65.6 19.6 %all-to-all-start.1 = ((f32[64,8,128]{2,1,0:T(8,128)}), f32[64,8,128]{2,1,0:T(8,128)S(1)}, u32[]{:S(2)}, u32[]{:S(2)}) async-start(f32[64,8,128]{2,1,0:T(8,128)} %bitcast.4), calls=%async_computation.1 | async-start | bytes 524288 | tf_op jit(solution)/shard_map/all_to_all | solution.py:412
  85.2 0.8 copy-start

commit v4 on v3

--- a/solution.py
+++ b/solution.py
@@ -17,7 +17,7 @@
 CAP = 3
 CHUNKS = CELLS // LANES
 BLOCK = CAP * CHUNKS
-BACK = 8
+BACK = CAP + 2
 NT = (((1,), (1,)), ((), ()))
 
 VM = pl.BlockSpec(memory_space=pltpu.VMEM)
@@ -94,12 +94,15 @@
 def build_side_matrix(taps, lhs, transposed, double):
     n = SIDE * HALF
     half = SIDE // 2 - 1
-    r = lax.broadcasted_iota(jnp.int32, (n, n), 0)
-    c = lax.broadcasted_iota(jnp.int32, (n, n), 1)
-    delta = jnp.right_shift(c, 3) - jnp.right_shift(r, 3)
-    offset = half - delta if transposed else delta + half
-    same = jnp.bitwise_and(r, HALF - 1) == jnp.bitwise_and(c, HALF - 1)
-    hi, lo = split2(tap_lookup(taps, jnp.where(same, offset, -1)))
+    a = lax.broadcasted_iota(jnp.int32, (SIDE, n), 0)
+    c = lax.broadcasted_iota(jnp.int32, (SIDE, n), 1)
+    delta = jnp.right_shift(c, 3) - a
+    pattern = tap_lookup(taps, half - delta if transposed else delta + half)
+    sub = lax.broadcasted_iota(jnp.int32, (HALF, n), 0)
+    lane = lax.broadcasted_iota(jnp.int32, (HALF, n), 1)
+    same = sub == jnp.bitwise_and(lane, HALF - 1)
+    full = jnp.concatenate([jnp.where(same, pattern[i : i + 1], 0.0) for i in range(SIDE)], axis=0)
+    hi, lo = split2(full)
     lhs[0:n, 0:n] = hi
     if not double:
         lhs[0:n, n : 2 * n] = lo
@@ -343,8 +346,6 @@
         out_ref[pl.ds(CAP + h, groups, stride=BACK), :] = jnp.broadcast_to(
             slab[:, h * LANES : (h + 1) * LANES], (groups, LANES)
         )
-    for s in range(CAP + 2, BACK):
-        out_ref[pl.ds(s, groups, stride=BACK), :] = jnp.zeros((groups, LANES), F32)
 
 
 def run_margin(received, owned, kernel_diag, slab, groups):
@@ -408,9 +409,10 @@
     upper = lax.ppermute(part[HALF:], "dom", [(i, (i + 1) % domains) for i in range(domains)])
     mine = lax.axis_index("grp") % HALF
     slab = lax.dynamic_slice_in_dim(part[:HALF] + upper, mine, 1, 0)
+    slab, select = lax.optimization_barrier((slab, select))
     products = run_margin(received, owned, kernel_diag, slab, groups)
     returned = lax.all_to_all(
-        products.reshape(groups, BACK, LANES), "grp", split_axis=0, concat_axis=0, tiled=True
+        products.reshape(groups, BACK, 1, LANES), "grp", split_axis=0, concat_axis=0, tiled=True
     )
     return run_gather(select, returned.reshape(groups * BACK, LANES), groups)
 

time: 87.4 us -> 84.1 us (0.962)
  blocking collectives: 0 us -> 17.9 us
  waiting for transfers between devices: 36.4 us -> 23.2 us
  starting transfers between devices: 33.6 us -> 27.2 us
    all_to_all x0 -> x1, blocking collectives: none -> 17.9 us  [body(): lax.all_to_all(products.reshape(groups, BACK, 1, LANES), 'grp', split_axi...]
    all_to_all x1 -> x0, waiting for transfers between devices: 11.7 us -> none  [body(): lax.all_to_all(products.reshape(groups, BACK, LANES), 'grp', split_axis=0...]
    all_to_all x1 -> x0, starting transfers between devices: 6.45 us -> none  [body(): lax.all_to_all(products.reshape(groups, BACK, LANES), 'grp', split_axis=0...]
    ppermute x1, waiting for transfers between devices: 8.77 us -> 7.25 us  [body(): lax.ppermute(part[HALF:], 'dom', [(i, (i + 1) % domains) for i in range(d...]
  transfers between devices with their start and end apart: 6 -> 5, of which waited for: 6 -> 5; matrix products, arithmetic and copies ran while one was open for 2% -> 2% of each run, Pallas kernels for 2% -> 2%
where the time goes in v4:
time: 84.1 us; the launch traced here: 83.7 us
  starting transfers between devices  27.2 us (32%)
  waiting for transfers between devices  23.2 us (28%)
  blocking collectives  17.9 us (21%)
  Pallas kernels  12.8 us (15%)
  other arithmetic  1.77 us (2%)
    all_to_all x1, blocking collectives, body(): lax.all_to_all(products.reshape(groups, BACK, 1, LANES), 'grp', split_axi...  17.9 us
    all_to_all x1, starting transfers between devices, body(): lax.all_to_all(outgoing, 'grp', split_axis=0, concat_axis=0, tiled=True)  14.6 us
    all_to_all x1, waiting for transfers between devices, body(): lax.all_to_all(outgoing, 'grp', split_axis=0, concat_axis=0, tiled=True)  11.9 us
    ppermute x3, starting transfers between devices, body(): lax.ppermute(part, 'grp', [(i, i ^ distance) for i in range(groups)])  10.6 us
    pallas_call x1, Pallas kernels, run_apply(): pl.pallas_call(functools.partial(apply_kernel, groups), out_shape=(jax.Sh...  9.34 us
    ppermute x1, waiting for transfers between devices, body(): lax.ppermute(part[HALF:], 'dom', [(i, (i + 1) % domains) for i in range(d...  7.25 us
    ppermute x3, waiting for transfers between devices, body(): lax.ppermute(part, 'grp', [(i, i ^ distance) for i in range(groups)])  4.03 us
    ppermute x1, starting transfers between devices, body(): lax.ppermute(part[HALF:], 'dom', [(i, (i + 1) % domains) for i in range(d...  1.91 us
  transfers between devices with their start and end apart: 5, of which 5 were waited for; matrix products, arithmetic and copies ran while one was open for 2% of the time, Pallas kernels for 2%

profile of v4, /device:TPU:1, one launch (start us, length us, event | category | flops | bytes accessed | tf_op | source)
XLA Modules:
  0.0 83.7 jit_solution(14518047120632285714)
XLA Ops:
  0.6 9.3 %apply.1 = (bf16[64,96,128]{2,1,0:T(8,128)(2,1)}, f32[16,256]{1,0:T(8,128)}) custom-call(f32[16]{0:T(128)} %magic_hbm.1, f32[16]{0:T(128)} %kinetic_hbm.1, f32[1,128]{1,0:T(1,128)} %bitcast.9, s32[1,128]{1,0:T(1,128)} %bitcast.11, f32[16,16,16,128]{3,2,1,0:T(8,128)} %x_hbm.1, f32[16,16,16,128]{3,2,1,0:T(8,128)} %pot_hbm.1), custom_call_target="tpu_custom_call" | custom-call | tf_op jit(solution)/shard_map/apply/pallas_call | solution.py:275
  10.0 0.0 copy-start.2
  10.0 14.6 %all-to-all-start = ((bf16[64,96,128]{2,1,0:T(8,128)(2,1)}), bf16[64,96,128]{2,1,0:T(8,128)(2,1)S(1)}, u32[]{:S(2)}, u32[]{:S(2)}) async-start(bf16[64,96,128]{2,1,0:T(8,128)(2,1)} %get-tuple-element.13), calls=%async_computation | async-start | bytes 3145728 | tf_op jit(solution)/shard_map/all_to_all | solution.py:401
  24.6 0.0 copy-start.1
  24.6 0.0 copy-done.2
  24.7 2.5 %collective-permute-start = (f32[16,256]{1,0:T(8,128)S(1)}, f32[16,256]{1,0:T(8,128)S(1)}, u32[]{:S(2)}, u32[]{:S(2)}) collective-permute-start(f32[16,256]{1,0:T(8,128)S(1)} %copy-done.2), channel_id=1, source_target_pairs={{0,1},{1,0},{2,3},{3,2},{4,5},{5,4},{6,7},{7,6},{8,9},{9,8},{10,11... | collective-permute-start | bytes 49160 | tf_op jit(solution)/shard_map/ppermute | solution.py:407
  27.1 0.8 collective-permute-done
  28.0 3.1 %collective-permute-start.1 = (f32[16,256]{1,0:T(8,128)S(1)}, f32[16,256]{1,0:T(8,128)S(1)}, u32[]{:S(2)}, u32[]{:S(2)}) collective-permute-start(f32[16,256]{1,0:T(8,128)S(1)} %add.19), channel_id=1, source_target_pairs={{0,2},{1,3},{2,0},{3,1},{4,6},{5,7},{6,4},{7,5},{8,10},{9,11},{10,... | collective-permute-start | bytes 49160 | tf_op jit(solution)/shard_map/ppermute | solution.py:407
  31.1 1.8 %collective-permute-done.1 = f32[16,256]{1,0:T(8,128)S(1)} collective-permute-done((f32[16,256]{1,0:T(8,128)S(1)}, f32[16,256]{1,0:T(8,128)S(1)}, u32[]{:S(2)}, u32[]{:S(2)}) %collective-permute-start.1) | collective-permute-done | bytes 16416 | tf_op jit(solution)/shard_map/ppermute | solution.py:407
  32.8 5.1 %collective-permute-start.2 = (f32[16,256]{1,0:T(8,128)S(1)}, f32[16,256]{1,0:T(8,128)S(1)}, u32[]{:S(2)}, u32[]{:S(2)}) collective-permute-start(f32[16,256]{1,0:T(8,128)S(1)} %add.20), channel_id=1, source_target_pairs={{0,4},{1,5},{2,6},{3,7},{4,0},{5,1},{6,2},{7,3},{8,12},{9,13},{10,... | collective-permute-start | bytes 49160 | tf_op jit(solution)/shard_map/ppermute | solution.py:407
  37.9 1.5 %collective-permute-done.2 = f32[16,256]{1,0:T(8,128)S(1)} collective-permute-done((f32[16,256]{1,0:T(8,128)S(1)}, f32[16,256]{1,0:T(8,128)S(1)}, u32[]{:S(2)}, u32[]{:S(2)}) %collective-permute-start.2) | collective-permute-done | bytes 16416 | tf_op jit(solution)/shard_map/ppermute | solution.py:407
  39.4 1.9 %collective-permute-start.3 = (f32[8,256]{1,0:T(8,128)S(1)}, f32[8,256]{1,0:T(8,128)S(1)}, u32[]{:S(2)}, u32[]{:S(2)}) collective-permute-start(f32[8,256]{1,0:T(8,128)S(1)} %get-tuple-element.17), channel_id=1, source_target_pairs={{0,64},{64,128},{128,192},{192,256},{256,320},{320,384},{384,448},... | collective-permute-start | bytes 24584 | tf_op jit(solution)/shard_map/ppermute | solution.py:409
  41.3 1.5 %select.3.select_ref = bf16[128,256]{1,0:T(8,128)(2,1)} custom-call(s32[1,128]{1,0:T(1,128)} %bitcast.12), custom_call_target="tpu_custom_call" | custom-call | tf_op jit(solution)/shard_map/select/pallas_call | solution.py:313
  42.8 1.8 %convert_element_type.5 = bf16[16,16,16,128]{3,2,1,0:T(8,128)(2,1)S(1)} convert(f32[16,16,16,128]{3,2,1,0:T(8,128)} %x_hbm.1) | non-fusion elementwise | flops 524288 | bytes 3145728 | tf_op jit(solution)/shard_map/convert_element_type | solution.py:404
  44.6 0.0 copy-start
  44.6 7.3 %collective-permute-done.3 = f32[8,256]{1,0:T(8,128)S(1)} collective-permute-done((f32[8,256]{1,0:T(8,128)S(1)}, f32[8,256]{1,0:T(8,128)S(1)}, u32[]{:S(2)}, u32[]{:S(2)}) %collective-permute-start.3) | collective-permute-done | bytes 8224 | tf_op jit(solution)/shard_map/ppermute | solution.py:409
  51.8 11.9 %all-to-all-done.recv_ref = bf16[64,96,128]{2,1,0:T(8,128)(2,1)S(1)} async-done(((bf16[64,96,128]{2,1,0:T(8,128)(2,1)}), bf16[64,96,128]{2,1,0:T(8,128)(2,1)S(1)}, u32[]{:S(2)}, u32[]{:S(2)}) %all-to-all-start) | async-done | bytes 1572896 | tf_op jit(solution)/shard_map/all_to_all | solution.py:401
  63.8 0.0 copy-done.1
  63.8 0.9 %margin.1 = f32[320,128]{1,0:T(8,128)S(1)} custom-call(bf16[64,96,128]{2,1,0:T(8,128)(2,1)S(1)} %all-to-all-done.recv_ref, bf16[4096,128]{1,0:T(8,128)(2,1)S(1)} %bitcast.6, f32[1,128]{1,0:T(1,128)S(1)} %bitcast.10, f32[1,256]{1,0:T(1,128)S(1)} %dynamic-slice_add_fusion.slab_ref), custom_call_target="tpu_custom_call" | custom-call | tf_op jit(solution)/shard_map/margin/pallas_call | solution.py:352
  64.7 17.9 %all_to_all.10 = f32[64,5,1,128]{3,2,1,0:T(1,128)S(1)} all-to-all(f32[64,5,1,128]{3,2,1,0:T(1,128)S(1)} %bitcast.7), channel_id=1, replica_groups=mesh['dom'=12,'grp'=64] {'grp'}, dimensions={0} | all-to-all | bytes 327680 | tf_op jit(solution)/shard_map/all_to_all | solution.py:414
  82.6 0.0 copy-done
  82.6 1.0 %gather.1 = (f32[128,128]{1,0:T(8,128)}, f32[8,256]{1,0:T(8,128)}) custom-call(bf16[128,256]{1,0:T(8,128)(2,1)S(1)} %copy-done, f32[320,128]{1,0:T(8,128)S(1)} %bitcast.8), custom_call_target="tpu_custom_call" | custom-call | tf_op jit(solution)/shard_map/gather/pallas_call | solution.py:380
  (5 shorter events, 0.0 us)
Async XLA Ops:
  10.0 14.7 %copy-start.2 = (f32[16,256]{1,0:T(8,128)S(1)}, f32[16,256]{1,0:T(8,128)}, u32[]{:S(2)}) copy-start(f32[16,256]{1,0:T(8,128)} %get-tuple-element.10) | copy-start | bytes 49156
  10.0 53.8 %all-to-all-start = ((bf16[64,96,128]{2,1,0:T(8,128)(2,1)}), bf16[64,96,128]{2,1,0:T(8,128)(2,1)S(1)}, u32[]{:S(2)}, u32[]{:S(2)}) async-start(bf16[64,96,128]{2,1,0:T(8,128)(2,1)} %get-tuple-element.13), calls=%async_computation | async-start | bytes 3145728 | tf_op jit(solution)/shard_map/all_to_all | solution.py:401
  24.6 39.1 %copy-start.1 = (f32[128]{0:T(128)S(1)}, f32[128]{0:T(128)}, u32[]{:S(2)}) copy-start(f32[128]{0:T(128)} %param.10) | copy-start | bytes 1540
  24.7 3.3 %collective-permute-start = (f32[16,256]{1,0:T(8,128)S(1)}, f32[16,256]{1,0:T(8,128)S(1)}, u32[]{:S(2)}, u32[]{:S(2)}) collective-permute-start(f32[16,256]{1,0:T(8,128)S(1)} %copy-done.2), channel_id=1, source_target_pairs={{0,1},{1,0},{2,3},{3,2},{4,5},{5,4},{6,7},{7,6},{8,9},{9,8},{10,11... | collective-permute-start | bytes 49160 | tf_op jit(solution)/shard_map/ppermute | solution.py:407
  28.0 4.8 %collective-permute-start.1 = (f32[16,256]{1,0:T(8,128)S(1)}, f32[16,256]{1,0:T(8,128)S(1)}, u32[]{:S(2)}, u32[]{:S(2)}) collective-permute-start(f32[16,256]{1,0:T(8,128)S(1)} %add.19), channel_id=1, source_target_pairs={{0,2},{1,3},{2,0},{3,1},{4,6},{5,7},{6,4},{7,5},{8,10},{9,11},{10,... | collective-permute-start | bytes 49160 | tf_op jit(solution)/shard_map/ppermute | solution.py:407
  32.8 6.5 %collective-permute-start.2 = (f32[16,256]{1,0:T(8,128)S(1)}, f32[16,256]{1,0:T(8,128)S(1)}, u32[]{:S(2)}, u32[]{:S(2)}) collective-permute-start(f32[16,256]{1,0:T(8,128)S(1)} %add.20), channel_id=1, source_target_pairs={{0,4},{1,5},{2,6},{3,7},{4,0},{5,1},{6,2},{7,3},{8,12},{9,13},{10,... | collective-permute-start | bytes 49160 | tf_op jit(solution)/shard_map/ppermute | solution.py:407
  39.4 12.5 %collective-permute-start.3 = (f32[8,256]{1,0:T(8,128)S(1)}, f32[8,256]{1,0:T(8,128)S(1)}, u32[]{:S(2)}, u32[]{:S(2)}) collective-permute-start(f32[8,256]{1,0:T(8,128)S(1)} %get-tuple-element.17), channel_id=1, source_target_pairs={{0,64},{64,128},{128,192},{192,256},{256,320},{320,384},{384,448},... | collective-permute-start | bytes 24584 | tf_op jit(solution)/shard_map/ppermute | solution.py:409
  44.6 38.1 %copy-start = (bf16[128,256]{1,0:T(8,128)(2,1)S(1)}, bf16[128,256]{1,0:T(8,128)(2,1)}, u32[]{:S(2)}) copy-start(bf16[128,256]{1,0:T(8,128)(2,1)} %select.3.select_ref) | copy-start | bytes 196612

commit v5 on v4

--- a/solution.py
+++ b/solution.py
@@ -56,39 +56,42 @@
     return jnp.sum(earlier, axis=0, keepdims=True).astype(jnp.int32)
 
 
-def build_plane_matrices(magic, kinetic, pat_ref, lhs1, lhs_b):
+def plane_patterns(taps, flip):
     half = SIDE // 2 - 1
     a = lax.broadcasted_iota(jnp.int32, (SIDE, PLANE), 0)
     c = lax.broadcasted_iota(jnp.int32, (SIDE, PLANE), 1)
     minor = jnp.bitwise_and(c, SIDE - 1) - a
     major = jnp.right_shift(c, 4) - a
-    f_minor = tap_lookup(magic, minor + half)
-    k_minor = tap_lookup(kinetic, minor + half)
-    ft_minor = tap_lookup(magic, half - minor)
-    pat_ref[0] = tap_lookup(magic, major + half)
-    pat_ref[1] = tap_lookup(kinetic, major + half)
-    pat_ref[2] = tap_lookup(magic, half - major)
-    same_minor = minor == 0
+    if flip:
+        minor, major = -minor, -major
+    return tap_lookup(taps, minor + half), tap_lookup(taps, major + half)
+
+
+def put_split(dst, row, mat, third):
+    hi, lo = split2(mat)
+    dst[row : row + SIDE, 0:PLANE] = hi
+    dst[row : row + SIDE, PLANE : 2 * PLANE] = lo
+    if third:
+        dst[row : row + SIDE, 2 * PLANE : 3 * PLANE] = hi
+
+
+def build_first(magic, kinetic, lhs1):
+    f_minor, f_major = plane_patterns(magic, False)
+    k_minor, k_major = plane_patterns(kinetic, False)
+    a = lax.broadcasted_iota(jnp.int32, (SIDE, PLANE), 0)
+    c = lax.broadcasted_iota(jnp.int32, (SIDE, PLANE), 1)
+    same_minor = jnp.bitwise_and(c, SIDE - 1) == a
     lane_major = jnp.right_shift(c, 4)
-
-    def put(dst, row, mat, third):
-        hi, lo = split2(mat)
-        dst[pl.ds(row, SIDE), 0:PLANE] = hi
-        dst[pl.ds(row, SIDE), PLANE : 2 * PLANE] = lo
-        if third:
-            dst[pl.ds(row, SIDE), 2 * PLANE : 3 * PLANE] = hi
-
-    def rows(g, carry):
-        r = pl.multiple_of(g * SIDE, SIDE)
-        fm = pat_ref[0, pl.ds(g, 1), :]
-        km = pat_ref[1, pl.ds(g, 1), :]
-        bm = pat_ref[2, pl.ds(g, 1), :]
-        put(lhs1, r, fm * f_minor, False)
-        put(lhs1, r + PLANE, jnp.where(same_minor, km, 0.0) + jnp.where(lane_major == g, k_minor, 0.0), False)
-        put(lhs_b, r, bm * ft_minor, True)
-        return carry
-
-    lax.fori_loop(0, SIDE, rows, 0)
+    for g in range(SIDE):
+        put_split(lhs1, g * SIDE, f_major[g : g + 1] * f_minor, False)
+        kin = jnp.where(same_minor, k_major[g : g + 1], 0.0) + jnp.where(lane_major == g, k_minor, 0.0)
+        put_split(lhs1, g * SIDE + PLANE, kin, False)
+
+
+def build_last(magic, lhs_b):
+    minor, major = plane_patterns(magic, True)
+    for g in range(SIDE):
+        put_split(lhs_b, g * SIDE, major[g : g + 1] * minor, True)
 
 
 def build_side_matrix(taps, lhs, transposed, double):
@@ -117,7 +120,7 @@
     magic_hbm, kinetic_hbm, diag_hbm, owner_hbm, x_hbm, pot_hbm,
     out_hbm, dens_ref,
     x_ref, pot_ref, z_ref, kin_ref, kin_i_ref, r_ref, v_ref,
-    pat_ref, lhs1, lhs_b, lhs_f, lhs_ft, lhs_k, sel_ref, rows_ref, stage_ref, grad_ref,
+    lhs1, lhs_b, lhs_f, lhs_ft, lhs_k, sel_ref, rows_ref, stage_ref, grad_ref,
     magic, kinetic, diag_ref, owner_ref,
     sem_s, sem_x, sem_p, sem_o,
 ):
@@ -139,14 +142,7 @@
     for c in small:
         c.wait()
 
-    build_plane_matrices(magic, kinetic, pat_ref, lhs1, lhs_b)
-    build_side_matrix(magic, lhs_f, False, True)
-    build_side_matrix(magic, lhs_ft, True, True)
-    build_side_matrix(kinetic, lhs_k, False, False)
-    owner = owner_ref[...]
-    column = slot_of(owner) * groups + owner
-    ri = lax.broadcasted_iota(jnp.int32, (CAP * groups, LANES), 0)
-    sel_ref[...] = jnp.where(ri == column, 1.0, 0.0).astype(BF16)
+    build_first(magic, kinetic, lhs1)
 
     def planes(ref, p):
         a, b = ref[2 * p], ref[2 * p + 1]
@@ -163,7 +159,21 @@
 
     for c in copies_x:
         c.wait()
-    lax.fori_loop(0, SIDE // 2, phase_a, 0, unroll=4)
+    for p in range(SIDE // 2):
+        phase_a(p, 0)
+        if p == 1:
+            build_side_matrix(magic, lhs_f, False, True)
+        if p == 2:
+            build_side_matrix(magic, lhs_ft, True, True)
+        if p == 3:
+            build_side_matrix(kinetic, lhs_k, False, False)
+        if p == 4:
+            build_last(magic, lhs_b)
+        if p == 5:
+            owner = owner_ref[...]
+            column = slot_of(owner) * groups + owner
+            ri = lax.broadcasted_iota(jnp.int32, (CAP * groups, LANES), 0)
+            sel_ref[...] = jnp.where(ri == column, 1.0, 0.0).astype(BF16)
     for c in copies_p:
         c.wait()
 
@@ -200,11 +210,12 @@
             total = total + jnp.where(here[None], d, 0.0)
         return total
 
-    filter_out(0)
+    for j in range(3):
+        filter_out(j)
     total = jnp.zeros((SIDE, HALF, LANES), F32)
     for j in range(SIDE):
-        if j + 1 < SIDE:
-            filter_out(j + 1)
+        if j + 3 < SIDE:
+            filter_out(j + 3)
         total = filter_back(j, total)
         if j % HALF == HALF - 1:
             t = j // HALF
@@ -236,29 +247,30 @@
                         t * 8 : t * 8 + 8, c * LANES : (c + 1) * LANES
                     ]
 
-    def stage(p, carry):
-        gradient(p)
-        dispatch(p - 1)
-        return carry
-
-    gradient(0)
-    for p in range(1, SIDE // 2):
-        stage(p, 0)
-    dispatch(SIDE // 2 - 1)
-    bands = 4
-    per = groups // bands
-
-    def pack(g):
+    def pack(g, half):
         tile, within = g // 8, g % 8
         for s in range(CAP):
             row = (s * (groups // 8) + tile) * (8 * CHUNKS) + within * 8
-            parts = [rows_ref[pl.ds(row + q * 64, 8), :] for q in range(CHUNKS // 8)]
-            stage_ref[g, s * CHUNKS : (s + 1) * CHUNKS, :] = jnp.concatenate(parts, axis=0).astype(BF16)
+            parts = [rows_ref[pl.ds(row + q * 64, 8), :] for q in (2 * half, 2 * half + 1)]
+            at = s * CHUNKS + half * CHUNKS // 2
+            stage_ref[g, at : at + CHUNKS // 2, :] = jnp.concatenate(parts, axis=0).astype(BF16)
+
+    bands = 4
+    per = groups // bands
+    steps = SIDE // 2
+    gradient(0)
+    for p in range(1, steps + 1):
+        if p < steps:
+            gradient(p)
+        dispatch(p - 1)
+        if p > steps // 2:
+            for g in range((p - 1 - steps // 2) * per, (p - steps // 2) * per):
+                pack(g, 0)
 
     outs = []
     for b in range(bands):
         for g in range(b * per, (b + 1) * per):
-            pack(g)
+            pack(g, 1)
         part = pl.ds(b * per, per)
         outs.append(pltpu.make_async_copy(stage_ref.at[part], out_hbm.at[part], sem_o.at[b]))
         outs[-1].start()
@@ -282,7 +294,6 @@
         out_specs=(HBM, VM),
         scratch_shapes=[
             box, box, box, box, slab, slab, slab,
-            pltpu.VMEM((3, SIDE, PLANE), F32),
             pltpu.VMEM((2 * PLANE, 2 * PLANE), BF16),
             pltpu.VMEM((PLANE, 3 * PLANE), BF16),
             side_lhs, side_lhs,
@@ -295,9 +306,12 @@
             pltpu.VMEM((1, LANES), F32), pltpu.VMEM((1, LANES), jnp.int32),
             dma, dma, dma, dma,
         ],
-        compiler_params=pltpu.CompilerParams(vmem_limit_bytes=67043328),
+        compiler_params=pltpu.CompilerParams(vmem_limit_bytes=48 * 1024 * 1024),
         name="apply",
-    )(magic_taps, kinetic_taps, kernel_diag.reshape(1, LANES), owners.reshape(1, LANES), support, potential)
+    )(*[
+        pltpu.with_memory_space_constraint(v, pltpu.HBM)
+        for v in (magic_taps, kinetic_taps, kernel_diag.reshape(1, LANES), owners.reshape(1, LANES), support, potential)
+    ])
 
 
 def select_kernel(groups, owner_ref, out_ref):

time: 84.1 us -> 82.9 us (0.986)
  Pallas kernels: 12.8 us -> 11.6 us
    pallas_call x1, Pallas kernels: 9.34 us -> 8.16 us  [run_apply(): pl.pallas_call(functools.partial(apply_kernel, groups), out_shape=(jax.Sh...]
where the time goes in v5:
time: 82.9 us; the launch traced here: 82.5 us
  starting transfers between devices  27.2 us (33%)
  waiting for transfers between devices  23.2 us (28%)
  blocking collectives  17.9 us (22%)
  Pallas kernels  11.6 us (14%)
  other arithmetic  1.77 us (2%)
    all_to_all x1, blocking collectives, body(): lax.all_to_all(products.reshape(groups, BACK, 1, LANES), 'grp', split_axi...  17.9 us
    all_to_all x1, starting transfers between devices, body(): lax.all_to_all(outgoing, 'grp', split_axis=0, concat_axis=0, tiled=True)  14.6 us
    all_to_all x1, waiting for transfers between devices, body(): lax.all_to_all(outgoing, 'grp', split_axis=0, concat_axis=0, tiled=True)  11.9 us
    ppermute x3, starting transfers between devices, body(): lax.ppermute(part, 'grp', [(i, i ^ distance) for i in range(groups)])  10.7 us
    pallas_call x1, Pallas kernels, run_apply(): pl.pallas_call(functools.partial(apply_kernel, groups), out_shape=(jax.Sh...  8.16 us
    ppermute x1, waiting for transfers between devices, body(): lax.ppermute(part[HALF:], 'dom', [(i, (i + 1) % domains) for i in range(d...  7.25 us
    ppermute x3, waiting for transfers between devices, body(): lax.ppermute(part, 'grp', [(i, i ^ distance) for i in range(groups)])  4 us
    ppermute x1, starting transfers between devices, body(): lax.ppermute(part[HALF:], 'dom', [(i, (i + 1) % domains) for i in range(d...  1.91 us
  transfers between devices with their start and end apart: 5, of which 5 were waited for; matrix products, arithmetic and copies ran while one was open for 2% of the time, Pallas kernels for 2%

profile of v5, /device:TPU:1, one launch (start us, length us, event | category | flops | bytes accessed | tf_op | source)
XLA Modules:
  0.0 82.5 jit_solution(11132295254226437210)
XLA Ops:
  0.6 8.2 %apply.1 = (bf16[64,96,128]{2,1,0:T(8,128)(2,1)}, f32[16,256]{1,0:T(8,128)S(1)}) custom-call(f32[16]{0:T(128)} %magic_hbm.1, f32[16]{0:T(128)} %kinetic_hbm.1, f32[1,128]{1,0:T(1,128)} %bitcast.9, s32[1,128]{1,0:T(1,128)} %bitcast.11, f32[16,16,16,128]{3,2,1,0:T(8,128)} %x_hbm.1, f32[16,16,16,128]{3,2,1,0:T(8,128)} %pot_hbm.1), custom_call_target="tpu_custom_call" | custom-call | tf_op jit(solution)/shard_map/apply/pallas_call | solution.py:287
  8.8 14.6 %all-to-all-start = ((bf16[64,96,128]{2,1,0:T(8,128)(2,1)}), bf16[64,96,128]{2,1,0:T(8,128)(2,1)S(1)}, u32[]{:S(2)}, u32[]{:S(2)}) async-start(bf16[64,96,128]{2,1,0:T(8,128)(2,1)} %get-tuple-element.13), calls=%async_computation | async-start | bytes 3145728 | tf_op jit(solution)/shard_map/all_to_all | solution.py:415
  23.4 0.0 copy-start.1
  23.5 2.5 %collective-permute-start = (f32[16,256]{1,0:T(8,128)S(1)}, f32[16,256]{1,0:T(8,128)S(1)}, u32[]{:S(2)}, u32[]{:S(2)}) collective-permute-start(f32[16,256]{1,0:T(8,128)S(1)} %get-tuple-element.10), channel_id=1, source_target_pairs={{0,1},{1,0},{2,3},{3,2},{4,5},{5,4},{6,7},{7,6},{8,9},{9,8},{10,11... | collective-permute-start | bytes 49160 | tf_op jit(solution)/shard_map/ppermute | solution.py:421
  25.9 0.8 collective-permute-done
  26.8 3.1 %collective-permute-start.1 = (f32[16,256]{1,0:T(8,128)S(1)}, f32[16,256]{1,0:T(8,128)S(1)}, u32[]{:S(2)}, u32[]{:S(2)}) collective-permute-start(f32[16,256]{1,0:T(8,128)S(1)} %add.19), channel_id=1, source_target_pairs={{0,2},{1,3},{2,0},{3,1},{4,6},{5,7},{6,4},{7,5},{8,10},{9,11},{10,... | collective-permute-start | bytes 49160 | tf_op jit(solution)/shard_map/ppermute | solution.py:421
  29.9 1.7 %collective-permute-done.1 = f32[16,256]{1,0:T(8,128)S(1)} collective-permute-done((f32[16,256]{1,0:T(8,128)S(1)}, f32[16,256]{1,0:T(8,128)S(1)}, u32[]{:S(2)}, u32[]{:S(2)}) %collective-permute-start.1) | collective-permute-done | bytes 16416 | tf_op jit(solution)/shard_map/ppermute | solution.py:421
  31.6 5.1 %collective-permute-start.2 = (f32[16,256]{1,0:T(8,128)S(1)}, f32[16,256]{1,0:T(8,128)S(1)}, u32[]{:S(2)}, u32[]{:S(2)}) collective-permute-start(f32[16,256]{1,0:T(8,128)S(1)} %add.20), channel_id=1, source_target_pairs={{0,4},{1,5},{2,6},{3,7},{4,0},{5,1},{6,2},{7,3},{8,12},{9,13},{10,... | collective-permute-start | bytes 49160 | tf_op jit(solution)/shard_map/ppermute | solution.py:421
  36.7 1.5 %collective-permute-done.2 = f32[16,256]{1,0:T(8,128)S(1)} collective-permute-done((f32[16,256]{1,0:T(8,128)S(1)}, f32[16,256]{1,0:T(8,128)S(1)}, u32[]{:S(2)}, u32[]{:S(2)}) %collective-permute-start.2) | collective-permute-done | bytes 16416 | tf_op jit(solution)/shard_map/ppermute | solution.py:421
  38.2 1.9 %collective-permute-start.3 = (f32[8,256]{1,0:T(8,128)S(1)}, f32[8,256]{1,0:T(8,128)S(1)}, u32[]{:S(2)}, u32[]{:S(2)}) collective-permute-start(f32[8,256]{1,0:T(8,128)S(1)} %get-tuple-element.17), channel_id=1, source_target_pairs={{0,64},{64,128},{128,192},{192,256},{256,320},{320,384},{384,448},... | collective-permute-start | bytes 24584 | tf_op jit(solution)/shard_map/ppermute | solution.py:423
  40.1 1.5 %select.3.select_ref = bf16[128,256]{1,0:T(8,128)(2,1)} custom-call(s32[1,128]{1,0:T(1,128)} %bitcast.12), custom_call_target="tpu_custom_call" | custom-call | tf_op jit(solution)/shard_map/select/pallas_call | solution.py:327
  41.6 1.8 %convert_element_type.5 = bf16[16,16,16,128]{3,2,1,0:T(8,128)(2,1)S(1)} convert(f32[16,16,16,128]{3,2,1,0:T(8,128)} %x_hbm.1) | non-fusion elementwise | flops 524288 | bytes 3145728 | tf_op jit(solution)/shard_map/convert_element_type | solution.py:418
  43.4 0.0 copy-start
  43.4 7.3 %collective-permute-done.3 = f32[8,256]{1,0:T(8,128)S(1)} collective-permute-done((f32[8,256]{1,0:T(8,128)S(1)}, f32[8,256]{1,0:T(8,128)S(1)}, u32[]{:S(2)}, u32[]{:S(2)}) %collective-permute-start.3) | collective-permute-done | bytes 8224 | tf_op jit(solution)/shard_map/ppermute | solution.py:423
  50.7 11.9 %all-to-all-done.recv_ref = bf16[64,96,128]{2,1,0:T(8,128)(2,1)S(1)} async-done(((bf16[64,96,128]{2,1,0:T(8,128)(2,1)}), bf16[64,96,128]{2,1,0:T(8,128)(2,1)S(1)}, u32[]{:S(2)}, u32[]{:S(2)}) %all-to-all-start) | async-done | bytes 1572896 | tf_op jit(solution)/shard_map/all_to_all | solution.py:415
  62.6 0.0 copy-done.1
  62.6 0.9 %margin.1 = f32[320,128]{1,0:T(8,128)S(1)} custom-call(bf16[64,96,128]{2,1,0:T(8,128)(2,1)S(1)} %all-to-all-done.recv_ref, bf16[4096,128]{1,0:T(8,128)(2,1)S(1)} %bitcast.6, f32[1,128]{1,0:T(1,128)S(1)} %bitcast.10, f32[1,256]{1,0:T(1,128)S(1)} %dynamic-slice_add_fusion.slab_ref), custom_call_target="tpu_custom_call" | custom-call | tf_op jit(solution)/shard_map/margin/pallas_call | solution.py:366
  63.5 17.9 %all_to_all.10 = f32[64,5,1,128]{3,2,1,0:T(1,128)S(1)} all-to-all(f32[64,5,1,128]{3,2,1,0:T(1,128)S(1)} %bitcast.7), channel_id=1, replica_groups=mesh['dom'=12,'grp'=64] {'grp'}, dimensions={0} | all-to-all | bytes 327680 | tf_op jit(solution)/shard_map/all_to_all | solution.py:428
  81.5 0.0 copy-done
  81.5 1.0 %gather.1 = (f32[128,128]{1,0:T(8,128)}, f32[8,256]{1,0:T(8,128)}) custom-call(bf16[128,256]{1,0:T(8,128)(2,1)S(1)} %copy-done, f32[320,128]{1,0:T(8,128)S(1)} %bitcast.8), custom_call_target="tpu_custom_call" | custom-call | tf_op jit(solution)/shard_map/gather/pallas_call | solution.py:394
  (5 shorter events, 0.0 us)
Async XLA Ops:
  8.8 53.8 %all-to-all-start = ((bf16[64,96,128]{2,1,0:T(8,128)(2,1)}), bf16[64,96,128]{2,1,0:T(8,128)(2,1)S(1)}, u32[]{:S(2)}, u32[]{:S(2)}) async-start(bf16[64,96,128]{2,1,0:T(8,128)(2,1)} %get-tuple-element.13), calls=%async_computation | async-start | bytes 3145728 | tf_op jit(solution)/shard_map/all_to_all | solution.py:415
  23.4 39.1 %copy-start.1 = (f32[128]{0:T(128)S(1)}, f32[128]{0:T(128)}, u32[]{:S(2)}) copy-start(f32[128]{0:T(128)} %param.10) | copy-start | bytes 1540
  23.5 3.3 %collective-permute-start = (f32[16,256]{1,0:T(8,128)S(1)}, f32[16,256]{1,0:T(8,128)S(1)}, u32[]{:S(2)}, u32[]{:S(2)}) collective-permute-start(f32[16,256]{1,0:T(8,128)S(1)} %get-tuple-element.10), channel_id=1, source_target_pairs={{0,1},{1,0},{2,3},{3,2},{4,5},{5,4},{6,7},{7,6},{8,9},{9,8},{10,11... | collective-permute-start | bytes 49160 | tf_op jit(solution)/shard_map/ppermute | solution.py:421
  26.8 4.8 %collective-permute-start.1 = (f32[16,256]{1,0:T(8,128)S(1)}, f32[16,256]{1,0:T(8,128)S(1)}, u32[]{:S(2)}, u32[]{:S(2)}) collective-permute-start(f32[16,256]{1,0:T(8,128)S(1)} %add.19), channel_id=1, source_target_pairs={{0,2},{1,3},{2,0},{3,1},{4,6},{5,7},{6,4},{7,5},{8,10},{9,11},{10,... | collective-permute-start | bytes 49160 | tf_op jit(solution)/shard_map/ppermute | solution.py:421
  31.6 6.6 %collective-permute-start.2 = (f32[16,256]{1,0:T(8,128)S(1)}, f32[16,256]{1,0:T(8,128)S(1)}, u32[]{:S(2)}, u32[]{:S(2)}) collective-permute-start(f32[16,256]{1,0:T(8,128)S(1)} %add.20), channel_id=1, source_target_pairs={{0,4},{1,5},{2,6},{3,7},{4,0},{5,1},{6,2},{7,3},{8,12},{9,13},{10,... | collective-permute-start | bytes 49160 | tf_op jit(solution)/shard_map/ppermute | solution.py:421
  38.2 12.5 %collective-permute-start.3 = (f32[8,256]{1,0:T(8,128)S(1)}, f32[8,256]{1,0:T(8,128)S(1)}, u32[]{:S(2)}, u32[]{:S(2)}) collective-permute-start(f32[8,256]{1,0:T(8,128)S(1)} %get-tuple-element.17), channel_id=1, source_target_pairs={{0,64},{64,128},{128,192},{192,256},{256,320},{320,384},{384,448},... | collective-permute-start | bytes 24584 | tf_op jit(solution)/shard_map/ppermute | solution.py:423
  43.4 38.1 %copy-start = (bf16[128,256]{1,0:T(8,128)(2,1)S(1)}, bf16[128,256]{1,0:T(8,128)(2,1)}, u32[]{:S(2)}) copy-start(bf16[128,256]{1,0:T(8,128)(2,1)} %select.3.select_ref) | copy-start | bytes 196612

commit v6 on v5

--- a/solution.py
+++ b/solution.py
@@ -17,7 +17,7 @@
 CAP = 3
 CHUNKS = CELLS // LANES
 BLOCK = CAP * CHUNKS
-BACK = CAP + 2
+BACK = CAP + 3
 NT = (((1,), (1,)), ((), ()))
 
 VM = pl.BlockSpec(memory_space=pltpu.VMEM)
@@ -69,10 +69,13 @@
 
 def put_split(dst, row, mat, third):
     hi, lo = split2(mat)
+    if not third:
+        dst[row : row + SIDE, :] = hi
+        dst[row + 2 * PLANE : row + 2 * PLANE + SIDE, :] = lo
+        return
     dst[row : row + SIDE, 0:PLANE] = hi
     dst[row : row + SIDE, PLANE : 2 * PLANE] = lo
-    if third:
-        dst[row : row + SIDE, 2 * PLANE : 3 * PLANE] = hi
+    dst[row : row + SIDE, 2 * PLANE : 3 * PLANE] = hi
 
 
 def build_first(magic, kinetic, lhs1):
@@ -149,8 +152,8 @@
         return jnp.concatenate([a.reshape(PLANE, LANES), b.reshape(PLANE, LANES)], axis=1)
 
     def phase_a(p, carry):
-        x = planes(x_ref, p).astype(BF16)
-        y = mm(lhs1[...], jnp.concatenate([x, x], axis=0))
+        y = mm(lhs1[...], planes(x_ref, p).astype(BF16))
+        y = y[: 2 * PLANE] + y[2 * PLANE :]
         for h in (0, 1):
             cols = slice(h * LANES, (h + 1) * LANES)
             z_ref[2 * p + h] = y[:PLANE, cols].reshape(SIDE, SIDE, LANES)
@@ -294,7 +297,7 @@
         out_specs=(HBM, VM),
         scratch_shapes=[
             box, box, box, box, slab, slab, slab,
-            pltpu.VMEM((2 * PLANE, 2 * PLANE), BF16),
+            pltpu.VMEM((4 * PLANE, PLANE), BF16),
             pltpu.VMEM((PLANE, 3 * PLANE), BF16),
             side_lhs, side_lhs,
             pltpu.VMEM((side, 2 * side), BF16),
@@ -333,7 +336,7 @@
     )(owners.reshape(1, LANES))
 
 
-def margin_kernel(groups, recv_ref, coef_ref, scale_ref, slab_ref, out_ref, rows_ref):
+def margin_kernel(groups, recv_ref, coef_ref, scale_ref, slab_ref, out_ref, rows_ref, back_ref):
     for g in range(groups):
         for s in range(CAP):
             block = recv_ref[g, s * CHUNKS : (s + 1) * CHUNKS, :].astype(F32)
@@ -354,36 +357,39 @@
         acc = acc + mm(lhs, coef_ref[i * PLANE : (i + 1) * PLANE, :])
     acc = acc * (scale_ref[...] * (1.0 / float(SIDE) ** 1.5))
     for s in range(CAP):
-        out_ref[pl.ds(s, groups, stride=BACK), :] = acc[s * groups : (s + 1) * groups]
+        back_ref[pl.ds(s, groups, stride=BACK), :] = acc[s * groups : (s + 1) * groups]
     slab = slab_ref[...]
     for h in range(2):
-        out_ref[pl.ds(CAP + h, groups, stride=BACK), :] = jnp.broadcast_to(
+        back_ref[pl.ds(CAP + h, groups, stride=BACK), :] = jnp.broadcast_to(
             slab[:, h * LANES : (h + 1) * LANES], (groups, LANES)
         )
+    back_ref[pl.ds(CAP + 2, groups, stride=BACK), :] = jnp.zeros((groups, LANES), F32)
+    out_ref[...] = back_ref[...].astype(BF16)
 
 
 def run_margin(received, owned, kernel_diag, slab, groups):
     return pl.pallas_call(
         functools.partial(margin_kernel, groups),
-        out_shape=jax.ShapeDtypeStruct((groups * BACK, LANES), F32),
+        out_shape=jax.ShapeDtypeStruct((groups * BACK, LANES), BF16),
         in_specs=[VM, VM, VM, VM],
         out_specs=VM,
-        scratch_shapes=[pltpu.VMEM((CAP * groups * CHUNKS, LANES), F32)],
+        scratch_shapes=[
+            pltpu.VMEM((CAP * groups * CHUNKS, LANES), F32),
+            pltpu.VMEM((groups * BACK, LANES), F32),
+        ],
         compiler_params=pltpu.CompilerParams(vmem_limit_bytes=16 * 1024 * 1024),
         name="margin",
     )(received, owned, kernel_diag.reshape(1, LANES), slab)
 
 
-def gather_kernel(groups, select_ref, ret_hbm, out_ref, dens_ref, ret_ref, sem):
+def gather_kernel(groups, select_ref, ret_hbm, out_ref, dens_ref, ret_ref, back_ref, sem):
     copy = pltpu.make_async_copy(ret_hbm, ret_ref, sem)
     copy.start()
     copy.wait()
-    rows = [ret_ref[pl.ds(s, groups, stride=BACK), :] for s in range(CAP + 2)]
+    back_ref[...] = ret_ref[...].astype(F32)
+    rows = [back_ref[pl.ds(s, groups, stride=BACK), :] for s in range(CAP + 2)]
     x = jnp.concatenate(rows[:CAP] + [jnp.zeros((groups, LANES), F32)], axis=0)
-    hi, mid = split2(x)
-    lo = (x - hi.astype(F32) - mid.astype(F32)).astype(BF16)
-    y = mm(select_ref[...], jnp.concatenate([hi, mid], axis=1))
-    out_ref[...] = y[:, :LANES] + (y[:, LANES:] + mm(select_ref[...], lo))
+    out_ref[...] = mm(select_ref[...], x.astype(BF16))
     for h in range(2):
         dens_ref[:, h * LANES : (h + 1) * LANES] = jnp.sum(
             rows[CAP + h].reshape(groups // HALF, HALF, LANES), axis=0
@@ -400,6 +406,7 @@
         in_specs=[VM, HBM],
         out_specs=(VM, VM),
         scratch_shapes=[
+            pltpu.VMEM((groups * BACK, LANES), BF16),
             pltpu.VMEM((groups * BACK, LANES), F32),
             pltpu.SemaphoreType.DMA,
         ],
@@ -426,7 +433,7 @@
     slab, select = lax.optimization_barrier((slab, select))
     products = run_margin(received, owned, kernel_diag, slab, groups)
     returned = lax.all_to_all(
-        products.reshape(groups, BACK, 1, LANES), "grp", split_axis=0, concat_axis=0, tiled=True
+        products.reshape(groups, BACK // 2, 2, LANES), "grp", split_axis=0, concat_axis=0, tiled=True
     )
     return run_gather(select, returned.reshape(groups * BACK, LANES), groups)
 

time: 82.9 us -> 81.7 us (0.986)
  blocking collectives: 17.9 us -> 16.8 us
    all_to_all x1, blocking collectives: 17.9 us -> 16.8 us  [body(): lax.all_to_all(products.reshape(groups, BACK // 2, 2, LANES), 'grp', spli...]
where the time goes in v6:
time: 81.7 us; the launch traced here: 81.3 us
  starting transfers between devices  27.2 us (33%)
  waiting for transfers between devices  23.2 us (28%)
  blocking collectives  16.8 us (21%)
  Pallas kernels  11.5 us (14%)
  other arithmetic  1.77 us (2%)
    all_to_all x1, blocking collectives, body(): lax.all_to_all(products.reshape(groups, BACK // 2, 2, LANES), 'grp', spli...  16.8 us
    all_to_all x1, starting transfers between devices, body(): lax.all_to_all(outgoing, 'grp', split_axis=0, concat_axis=0, tiled=True)  14.6 us
    all_to_all x1, waiting for transfers between devices, body(): lax.all_to_all(outgoing, 'grp', split_axis=0, concat_axis=0, tiled=True)  11.9 us
    ppermute x3, starting transfers between devices, body(): lax.ppermute(part, 'grp', [(i, i ^ distance) for i in range(groups)])  10.7 us
    pallas_call x1, Pallas kernels, run_apply(): pl.pallas_call(functools.partial(apply_kernel, groups), out_shape=(jax.Sh...  8.17 us
    ppermute x1, waiting for transfers between devices, body(): lax.ppermute(part[HALF:], 'dom', [(i, (i + 1) % domains) for i in range(d...  7.25 us
    ppermute x3, waiting for transfers between devices, body(): lax.ppermute(part, 'grp', [(i, i ^ distance) for i in range(groups)])  4 us
    ppermute x1, starting transfers between devices, body(): lax.ppermute(part[HALF:], 'dom', [(i, (i + 1) % domains) for i in range(d...  1.91 us
  transfers between devices with their start and end apart: 5, of which 5 were waited for; matrix products, arithmetic and copies ran while one was open for 2% of the time, Pallas kernels for 2%

profile of v6, /device:TPU:1, one launch (start us, length us, event | category | flops | bytes accessed | tf_op | source)
XLA Modules:
  0.0 81.3 jit_solution(4280198116376586040)
XLA Ops:
  0.6 8.2 %apply.1 = (bf16[64,96,128]{2,1,0:T(8,128)(2,1)}, f32[16,256]{1,0:T(8,128)S(1)}) custom-call(f32[16]{0:T(128)} %magic_hbm.1, f32[16]{0:T(128)} %kinetic_hbm.1, f32[1,128]{1,0:T(1,128)} %bitcast.9, s32[1,128]{1,0:T(1,128)} %bitcast.11, f32[16,16,16,128]{3,2,1,0:T(8,128)} %x_hbm.1, f32[16,16,16,128]{3,2,1,0:T(8,128)} %pot_hbm.1), custom_call_target="tpu_custom_call" | custom-call | tf_op jit(solution)/shard_map/apply/pallas_call | solution.py:290
  8.8 14.6 %all-to-all-start = ((bf16[64,96,128]{2,1,0:T(8,128)(2,1)}), bf16[64,96,128]{2,1,0:T(8,128)(2,1)S(1)}, u32[]{:S(2)}, u32[]{:S(2)}) async-start(bf16[64,96,128]{2,1,0:T(8,128)(2,1)} %get-tuple-element.13), calls=%async_computation | async-start | bytes 3145728 | tf_op jit(solution)/shard_map/all_to_all | solution.py:422
  23.4 0.0 copy-start.1
  23.5 2.5 %collective-permute-start = (f32[16,256]{1,0:T(8,128)S(1)}, f32[16,256]{1,0:T(8,128)S(1)}, u32[]{:S(2)}, u32[]{:S(2)}) collective-permute-start(f32[16,256]{1,0:T(8,128)S(1)} %get-tuple-element.10), channel_id=1, source_target_pairs={{0,1},{1,0},{2,3},{3,2},{4,5},{5,4},{6,7},{7,6},{8,9},{9,8},{10,11... | collective-permute-start | bytes 49160 | tf_op jit(solution)/shard_map/ppermute | solution.py:428
  25.9 0.8 %collective-permute-done = f32[16,256]{1,0:T(8,128)S(1)} collective-permute-done((f32[16,256]{1,0:T(8,128)S(1)}, f32[16,256]{1,0:T(8,128)S(1)}, u32[]{:S(2)}, u32[]{:S(2)}) %collective-permute-start) | collective-permute-done | bytes 16416 | tf_op jit(solution)/shard_map/ppermute | solution.py:428
  26.8 3.1 %collective-permute-start.1 = (f32[16,256]{1,0:T(8,128)S(1)}, f32[16,256]{1,0:T(8,128)S(1)}, u32[]{:S(2)}, u32[]{:S(2)}) collective-permute-start(f32[16,256]{1,0:T(8,128)S(1)} %add.19), channel_id=1, source_target_pairs={{0,2},{1,3},{2,0},{3,1},{4,6},{5,7},{6,4},{7,5},{8,10},{9,11},{10,... | collective-permute-start | bytes 49160 | tf_op jit(solution)/shard_map/ppermute | solution.py:428
  29.9 1.7 %collective-permute-done.1 = f32[16,256]{1,0:T(8,128)S(1)} collective-permute-done((f32[16,256]{1,0:T(8,128)S(1)}, f32[16,256]{1,0:T(8,128)S(1)}, u32[]{:S(2)}, u32[]{:S(2)}) %collective-permute-start.1) | collective-permute-done | bytes 16416 | tf_op jit(solution)/shard_map/ppermute | solution.py:428
  31.6 5.1 %collective-permute-start.2 = (f32[16,256]{1,0:T(8,128)S(1)}, f32[16,256]{1,0:T(8,128)S(1)}, u32[]{:S(2)}, u32[]{:S(2)}) collective-permute-start(f32[16,256]{1,0:T(8,128)S(1)} %add.20), channel_id=1, source_target_pairs={{0,4},{1,5},{2,6},{3,7},{4,0},{5,1},{6,2},{7,3},{8,12},{9,13},{10,... | collective-permute-start | bytes 49160 | tf_op jit(solution)/shard_map/ppermute | solution.py:428
  36.7 1.5 %collective-permute-done.2 = f32[16,256]{1,0:T(8,128)S(1)} collective-permute-done((f32[16,256]{1,0:T(8,128)S(1)}, f32[16,256]{1,0:T(8,128)S(1)}, u32[]{:S(2)}, u32[]{:S(2)}) %collective-permute-start.2) | collective-permute-done | bytes 16416 | tf_op jit(solution)/shard_map/ppermute | solution.py:428
  38.2 1.9 %collective-permute-start.3 = (f32[8,256]{1,0:T(8,128)S(1)}, f32[8,256]{1,0:T(8,128)S(1)}, u32[]{:S(2)}, u32[]{:S(2)}) collective-permute-start(f32[8,256]{1,0:T(8,128)S(1)} %get-tuple-element.17), channel_id=1, source_target_pairs={{0,64},{64,128},{128,192},{192,256},{256,320},{320,384},{384,448},... | collective-permute-start | bytes 24584 | tf_op jit(solution)/shard_map/ppermute | solution.py:430
  40.1 1.5 %select.3.select_ref = bf16[128,256]{1,0:T(8,128)(2,1)} custom-call(s32[1,128]{1,0:T(1,128)} %bitcast.12), custom_call_target="tpu_custom_call" | custom-call | tf_op jit(solution)/shard_map/select/pallas_call | solution.py:330
  41.6 1.8 %convert_element_type.5 = bf16[16,16,16,128]{3,2,1,0:T(8,128)(2,1)S(1)} convert(f32[16,16,16,128]{3,2,1,0:T(8,128)} %x_hbm.1) | non-fusion elementwise | flops 524288 | bytes 3145728 | tf_op jit(solution)/shard_map/convert_element_type | solution.py:425
  43.4 0.0 copy-start
  43.4 7.3 %collective-permute-done.3 = f32[8,256]{1,0:T(8,128)S(1)} collective-permute-done((f32[8,256]{1,0:T(8,128)S(1)}, f32[8,256]{1,0:T(8,128)S(1)}, u32[]{:S(2)}, u32[]{:S(2)}) %collective-permute-start.3) | collective-permute-done | bytes 8224 | tf_op jit(solution)/shard_map/ppermute | solution.py:430
  50.6 11.9 %all-to-all-done.recv_ref = bf16[64,96,128]{2,1,0:T(8,128)(2,1)S(1)} async-done(((bf16[64,96,128]{2,1,0:T(8,128)(2,1)}), bf16[64,96,128]{2,1,0:T(8,128)(2,1)S(1)}, u32[]{:S(2)}, u32[]{:S(2)}) %all-to-all-start) | async-done | bytes 1572896 | tf_op jit(solution)/shard_map/all_to_all | solution.py:422
  62.6 0.0 copy-done.1
  62.6 0.9 %margin.1 = bf16[384,128]{1,0:T(8,128)(2,1)S(1)} custom-call(bf16[64,96,128]{2,1,0:T(8,128)(2,1)S(1)} %all-to-all-done.recv_ref, bf16[4096,128]{1,0:T(8,128)(2,1)S(1)} %bitcast.6, f32[1,128]{1,0:T(1,128)S(1)} %bitcast.10, f32[1,256]{1,0:T(1,128)S(1)} %dynamic-slice_add_fusion.slab_ref), custom_call_target="tpu_custom_call" | custom-call | tf_op jit(solution)/shard_map/margin/pallas_call | solution.py:371
  63.5 16.8 %all_to_all.10 = bf16[64,3,2,128]{3,2,1,0:T(2,128)(2,1)S(1)} all-to-all(bf16[64,3,2,128]{3,2,1,0:T(2,128)(2,1)S(1)} %bitcast.7), channel_id=1, replica_groups=mesh['dom'=12,'grp'=64] {'grp'}, dimensions={0} | all-to-all | bytes 196608 | tf_op jit(solution)/shard_map/all_to_all | solution.py:435
  80.3 0.0 copy-done
  80.3 0.9 %gather.1 = (f32[128,128]{1,0:T(8,128)}, f32[8,256]{1,0:T(8,128)}) custom-call(bf16[128,256]{1,0:T(8,128)(2,1)S(1)} %copy-done, bf16[384,128]{1,0:T(8,128)(2,1)S(1)} %bitcast.8), custom_call_target="tpu_custom_call" | custom-call | tf_op jit(solution)/shard_map/gather/pallas_call | solution.py:400
  (5 shorter events, 0.0 us)
Async XLA Ops:
  8.8 53.8 %all-to-all-start = ((bf16[64,96,128]{2,1,0:T(8,128)(2,1)}), bf16[64,96,128]{2,1,0:T(8,128)(2,1)S(1)}, u32[]{:S(2)}, u32[]{:S(2)}) async-start(bf16[64,96,128]{2,1,0:T(8,128)(2,1)} %get-tuple-element.13), calls=%async_computation | async-start | bytes 3145728 | tf_op jit(solution)/shard_map/all_to_all | solution.py:422
  23.4 39.1 %copy-start.1 = (f32[128]{0:T(128)S(1)}, f32[128]{0:T(128)}, u32[]{:S(2)}) copy-start(f32[128]{0:T(128)} %param.10) | copy-start | bytes 1540
  23.5 3.3 %collective-permute-start = (f32[16,256]{1,0:T(8,128)S(1)}, f32[16,256]{1,0:T(8,128)S(1)}, u32[]{:S(2)}, u32[]{:S(2)}) collective-permute-start(f32[16,256]{1,0:T(8,128)S(1)} %get-tuple-element.10), channel_id=1, source_target_pairs={{0,1},{1,0},{2,3},{3,2},{4,5},{5,4},{6,7},{7,6},{8,9},{9,8},{10,11... | collective-permute-start | bytes 49160 | tf_op jit(solution)/shard_map/ppermute | solution.py:428
  26.8 4.8 %collective-permute-start.1 = (f32[16,256]{1,0:T(8,128)S(1)}, f32[16,256]{1,0:T(8,128)S(1)}, u32[]{:S(2)}, u32[]{:S(2)}) collective-permute-start(f32[16,256]{1,0:T(8,128)S(1)} %add.19), channel_id=1, source_target_pairs={{0,2},{1,3},{2,0},{3,1},{4,6},{5,7},{6,4},{7,5},{8,10},{9,11},{10,... | collective-permute-start | bytes 49160 | tf_op jit(solution)/shard_map/ppermute | solution.py:428
  31.6 6.6 %collective-permute-start.2 = (f32[16,256]{1,0:T(8,128)S(1)}, f32[16,256]{1,0:T(8,128)S(1)}, u32[]{:S(2)}, u32[]{:S(2)}) collective-permute-start(f32[16,256]{1,0:T(8,128)S(1)} %add.20), channel_id=1, source_target_pairs={{0,4},{1,5},{2,6},{3,7},{4,0},{5,1},{6,2},{7,3},{8,12},{9,13},{10,... | collective-permute-start | bytes 49160 | tf_op jit(solution)/shard_map/ppermute | solution.py:428
  38.2 12.5 %collective-permute-start.3 = (f32[8,256]{1,0:T(8,128)S(1)}, f32[8,256]{1,0:T(8,128)S(1)}, u32[]{:S(2)}, u32[]{:S(2)}) collective-permute-start(f32[8,256]{1,0:T(8,128)S(1)} %get-tuple-element.17), channel_id=1, source_target_pairs={{0,64},{64,128},{128,192},{192,256},{256,320},{320,384},{384,448},... | collective-permute-start | bytes 24584 | tf_op jit(solution)/shard_map/ppermute | solution.py:430
  43.4 37.0 %copy-start = (bf16[128,256]{1,0:T(8,128)(2,1)S(1)}, bf16[128,256]{1,0:T(8,128)(2,1)}, u32[]{:S(2)}) copy-start(bf16[128,256]{1,0:T(8,128)(2,1)} %select.3.select_ref) | copy-start | bytes 196612

commit v7 on v6

--- a/solution.py
+++ b/solution.py
@@ -261,6 +261,14 @@
     bands = 4
     per = groups // bands
     steps = SIDE // 2
+    outs = []
+
+    def send(first, count, half):
+        for s in range(CAP):
+            part = (pl.ds(first, count), pl.ds(s * CHUNKS + half * CHUNKS // 2, CHUNKS // 2))
+            outs.append(pltpu.make_async_copy(stage_ref.at[part], out_hbm.at[part], sem_o.at[len(outs)]))
+            outs[-1].start()
+
     gradient(0)
     for p in range(1, steps + 1):
         if p < steps:
@@ -269,14 +277,14 @@
         if p > steps // 2:
             for g in range((p - 1 - steps // 2) * per, (p - steps // 2) * per):
                 pack(g, 0)
-
-    outs = []
+        if p == steps - 1:
+            send(0, 3 * per, 0)
+    send(3 * per, per, 0)
+
     for b in range(bands):
         for g in range(b * per, (b + 1) * per):
             pack(g, 1)
-        part = pl.ds(b * per, per)
-        outs.append(pltpu.make_async_copy(stage_ref.at[part], out_hbm.at[part], sem_o.at[b]))
-        outs[-1].start()
+        send(b * per, per, 1)
     for c in outs:
         c.wait()
 
@@ -307,7 +315,7 @@
             pltpu.VMEM((SIDE // 2, PLANE, 2 * LANES), BF16),
             pltpu.SMEM((SIDE,), F32), pltpu.SMEM((SIDE,), F32),
             pltpu.VMEM((1, LANES), F32), pltpu.VMEM((1, LANES), jnp.int32),
-            dma, dma, dma, dma,
+            dma, dma, dma, pltpu.SemaphoreType.DMA((CAP * 6,)),
         ],
         compiler_params=pltpu.CompilerParams(vmem_limit_bytes=48 * 1024 * 1024),
         name="apply",

time: 81.7 us -> 81.5 us (level)
  no operation moved by 1% of the time
where the time goes in v7:
time: 81.5 us; the launch traced here: 81.1 us
  starting transfers between devices  27.2 us (33%)
  waiting for transfers between devices  23.2 us (28%)
  blocking collectives  16.8 us (21%)
  Pallas kernels  11.4 us (14%)
  other arithmetic  1.77 us (2%)
    all_to_all x1, blocking collectives, body(): lax.all_to_all(products.reshape(groups, BACK // 2, 2, LANES), 'grp', spli...  16.8 us
    all_to_all x1, starting transfers between devices, body(): lax.all_to_all(outgoing, 'grp', split_axis=0, concat_axis=0, tiled=True)  14.6 us
    all_to_all x1, waiting for transfers between devices, body(): lax.all_to_all(outgoing, 'grp', split_axis=0, concat_axis=0, tiled=True)  11.9 us
    ppermute x3, starting transfers between devices, body(): lax.ppermute(part, 'grp', [(i, i ^ distance) for i in range(groups)])  10.7 us
    pallas_call x1, Pallas kernels, run_apply(): pl.pallas_call(functools.partial(apply_kernel, groups), out_shape=(jax.Sh...  8.06 us
    ppermute x1, waiting for transfers between devices, body(): lax.ppermute(part[HALF:], 'dom', [(i, (i + 1) % domains) for i in range(d...  7.25 us
    ppermute x3, waiting for transfers between devices, body(): lax.ppermute(part, 'grp', [(i, i ^ distance) for i in range(groups)])  4 us
    ppermute x1, starting transfers between devices, body(): lax.ppermute(part[HALF:], 'dom', [(i, (i + 1) % domains) for i in range(d...  1.91 us
  transfers between devices with their start and end apart: 5, of which 5 were waited for; matrix products, arithmetic and copies ran while one was open for 2% of the time, Pallas kernels for 2%

profile of v7, /device:TPU:1, one launch (start us, length us, event | category | flops | bytes accessed | tf_op | source)
XLA Modules:
  0.0 81.1 jit_solution(9567517016267333807)
XLA Ops:
  0.6 8.1 %apply.1 = (bf16[64,96,128]{2,1,0:T(8,128)(2,1)}, f32[16,256]{1,0:T(8,128)S(1)}) custom-call(f32[16]{0:T(128)} %magic_hbm.1, f32[16]{0:T(128)} %kinetic_hbm.1, f32[1,128]{1,0:T(1,128)} %bitcast.9, s32[1,128]{1,0:T(1,128)} %bitcast.11, f32[16,16,16,128]{3,2,1,0:T(8,128)} %x_hbm.1, f32[16,16,16,128]{3,2,1,0:T(8,128)} %pot_hbm.1), custom_call_target="tpu_custom_call" | custom-call | tf_op jit(solution)/shard_map/apply/pallas_call | solution.py:298
  8.7 14.6 %all-to-all-start = ((bf16[64,96,128]{2,1,0:T(8,128)(2,1)}), bf16[64,96,128]{2,1,0:T(8,128)(2,1)S(1)}, u32[]{:S(2)}, u32[]{:S(2)}) async-start(bf16[64,96,128]{2,1,0:T(8,128)(2,1)} %get-tuple-element.13), calls=%async_computation | async-start | bytes 3145728 | tf_op jit(solution)/shard_map/all_to_all | solution.py:430
  23.3 0.0 copy-start.1
  23.3 2.5 %collective-permute-start = (f32[16,256]{1,0:T(8,128)S(1)}, f32[16,256]{1,0:T(8,128)S(1)}, u32[]{:S(2)}, u32[]{:S(2)}) collective-permute-start(f32[16,256]{1,0:T(8,128)S(1)} %get-tuple-element.10), channel_id=1, source_target_pairs={{0,1},{1,0},{2,3},{3,2},{4,5},{5,4},{6,7},{7,6},{8,9},{9,8},{10,11... | collective-permute-start | bytes 49160 | tf_op jit(solution)/shard_map/ppermute | solution.py:436
  25.8 0.8 %collective-permute-done = f32[16,256]{1,0:T(8,128)S(1)} collective-permute-done((f32[16,256]{1,0:T(8,128)S(1)}, f32[16,256]{1,0:T(8,128)S(1)}, u32[]{:S(2)}, u32[]{:S(2)}) %collective-permute-start) | collective-permute-done | bytes 16416 | tf_op jit(solution)/shard_map/ppermute | solution.py:436
  26.6 3.1 %collective-permute-start.1 = (f32[16,256]{1,0:T(8,128)S(1)}, f32[16,256]{1,0:T(8,128)S(1)}, u32[]{:S(2)}, u32[]{:S(2)}) collective-permute-start(f32[16,256]{1,0:T(8,128)S(1)} %add.19), channel_id=1, source_target_pairs={{0,2},{1,3},{2,0},{3,1},{4,6},{5,7},{6,4},{7,5},{8,10},{9,11},{10,... | collective-permute-start | bytes 49160 | tf_op jit(solution)/shard_map/ppermute | solution.py:436
  29.7 1.7 %collective-permute-done.1 = f32[16,256]{1,0:T(8,128)S(1)} collective-permute-done((f32[16,256]{1,0:T(8,128)S(1)}, f32[16,256]{1,0:T(8,128)S(1)}, u32[]{:S(2)}, u32[]{:S(2)}) %collective-permute-start.1) | collective-permute-done | bytes 16416 | tf_op jit(solution)/shard_map/ppermute | solution.py:436
  31.5 5.1 %collective-permute-start.2 = (f32[16,256]{1,0:T(8,128)S(1)}, f32[16,256]{1,0:T(8,128)S(1)}, u32[]{:S(2)}, u32[]{:S(2)}) collective-permute-start(f32[16,256]{1,0:T(8,128)S(1)} %add.20), channel_id=1, source_target_pairs={{0,4},{1,5},{2,6},{3,7},{4,0},{5,1},{6,2},{7,3},{8,12},{9,13},{10,... | collective-permute-start | bytes 49160 | tf_op jit(solution)/shard_map/ppermute | solution.py:436
  36.6 1.5 %collective-permute-done.2 = f32[16,256]{1,0:T(8,128)S(1)} collective-permute-done((f32[16,256]{1,0:T(8,128)S(1)}, f32[16,256]{1,0:T(8,128)S(1)}, u32[]{:S(2)}, u32[]{:S(2)}) %collective-permute-start.2) | collective-permute-done | bytes 16416 | tf_op jit(solution)/shard_map/ppermute | solution.py:436
  38.1 1.9 %collective-permute-start.3 = (f32[8,256]{1,0:T(8,128)S(1)}, f32[8,256]{1,0:T(8,128)S(1)}, u32[]{:S(2)}, u32[]{:S(2)}) collective-permute-start(f32[8,256]{1,0:T(8,128)S(1)} %get-tuple-element.17), channel_id=1, source_target_pairs={{0,64},{64,128},{128,192},{192,256},{256,320},{320,384},{384,448},... | collective-permute-start | bytes 24584 | tf_op jit(solution)/shard_map/ppermute | solution.py:438
  40.0 1.5 %select.3.select_ref = bf16[128,256]{1,0:T(8,128)(2,1)} custom-call(s32[1,128]{1,0:T(1,128)} %bitcast.12), custom_call_target="tpu_custom_call" | custom-call | tf_op jit(solution)/shard_map/select/pallas_call | solution.py:338
  41.5 1.8 %convert_element_type.5 = bf16[16,16,16,128]{3,2,1,0:T(8,128)(2,1)S(1)} convert(f32[16,16,16,128]{3,2,1,0:T(8,128)} %x_hbm.1) | non-fusion elementwise | flops 524288 | bytes 3145728 | tf_op jit(solution)/shard_map/convert_element_type | solution.py:433
  43.3 0.0 copy-start
  43.3 7.3 %collective-permute-done.3 = f32[8,256]{1,0:T(8,128)S(1)} collective-permute-done((f32[8,256]{1,0:T(8,128)S(1)}, f32[8,256]{1,0:T(8,128)S(1)}, u32[]{:S(2)}, u32[]{:S(2)}) %collective-permute-start.3) | collective-permute-done | bytes 8224 | tf_op jit(solution)/shard_map/ppermute | solution.py:438
  50.5 11.9 %all-to-all-done.recv_ref = bf16[64,96,128]{2,1,0:T(8,128)(2,1)S(1)} async-done(((bf16[64,96,128]{2,1,0:T(8,128)(2,1)}), bf16[64,96,128]{2,1,0:T(8,128)(2,1)S(1)}, u32[]{:S(2)}, u32[]{:S(2)}) %all-to-all-start) | async-done | bytes 1572896 | tf_op jit(solution)/shard_map/all_to_all | solution.py:430
  62.4 0.0 copy-done.1
  62.5 0.9 %margin.1 = bf16[384,128]{1,0:T(8,128)(2,1)S(1)} custom-call(bf16[64,96,128]{2,1,0:T(8,128)(2,1)S(1)} %all-to-all-done.recv_ref, bf16[4096,128]{1,0:T(8,128)(2,1)S(1)} %bitcast.6, f32[1,128]{1,0:T(1,128)S(1)} %bitcast.10, f32[1,256]{1,0:T(1,128)S(1)} %dynamic-slice_add_fusion.slab_ref), custom_call_target="tpu_custom_call" | custom-call | tf_op jit(solution)/shard_map/margin/pallas_call | solution.py:379
  63.4 16.8 %all_to_all.10 = bf16[64,3,2,128]{3,2,1,0:T(2,128)(2,1)S(1)} all-to-all(bf16[64,3,2,128]{3,2,1,0:T(2,128)(2,1)S(1)} %bitcast.7), channel_id=1, replica_groups=mesh['dom'=12,'grp'=64] {'grp'}, dimensions={0} | all-to-all | bytes 196608 | tf_op jit(solution)/shard_map/all_to_all | solution.py:443
  80.2 0.0 copy-done
  80.2 0.9 %gather.1 = (f32[128,128]{1,0:T(8,128)}, f32[8,256]{1,0:T(8,128)}) custom-call(bf16[128,256]{1,0:T(8,128)(2,1)S(1)} %copy-done, bf16[384,128]{1,0:T(8,128)(2,1)S(1)} %bitcast.8), custom_call_target="tpu_custom_call" | custom-call | tf_op jit(solution)/shard_map/gather/pallas_call | solution.py:408
  (5 shorter events, 0.0 us)
Async XLA Ops:
  8.7 53.7 %all-to-all-start = ((bf16[64,96,128]{2,1,0:T(8,128)(2,1)}), bf16[64,96,128]{2,1,0:T(8,128)(2,1)S(1)}, u32[]{:S(2)}, u32[]{:S(2)}) async-start(bf16[64,96,128]{2,1,0:T(8,128)(2,1)} %get-tuple-element.13), calls=%async_computation | async-start | bytes 3145728 | tf_op jit(solution)/shard_map/all_to_all | solution.py:430
  23.3 39.1 %copy-start.1 = (f32[128]{0:T(128)S(1)}, f32[128]{0:T(128)}, u32[]{:S(2)}) copy-start(f32[128]{0:T(128)} %param.10) | copy-start | bytes 1540
  23.3 3.3 %collective-permute-start = (f32[16,256]{1,0:T(8,128)S(1)}, f32[16,256]{1,0:T(8,128)S(1)}, u32[]{:S(2)}, u32[]{:S(2)}) collective-permute-start(f32[16,256]{1,0:T(8,128)S(1)} %get-tuple-element.10), channel_id=1, source_target_pairs={{0,1},{1,0},{2,3},{3,2},{4,5},{5,4},{6,7},{7,6},{8,9},{9,8},{10,11... | collective-permute-start | bytes 49160 | tf_op jit(solution)/shard_map/ppermute | solution.py:436
  26.6 4.8 %collective-permute-start.1 = (f32[16,256]{1,0:T(8,128)S(1)}, f32[16,256]{1,0:T(8,128)S(1)}, u32[]{:S(2)}, u32[]{:S(2)}) collective-permute-start(f32[16,256]{1,0:T(8,128)S(1)} %add.19), channel_id=1, source_target_pairs={{0,2},{1,3},{2,0},{3,1},{4,6},{5,7},{6,4},{7,5},{8,10},{9,11},{10,... | collective-permute-start | bytes 49160 | tf_op jit(solution)/shard_map/ppermute | solution.py:436
  31.5 6.6 %collective-permute-start.2 = (f32[16,256]{1,0:T(8,128)S(1)}, f32[16,256]{1,0:T(8,128)S(1)}, u32[]{:S(2)}, u32[]{:S(2)}) collective-permute-start(f32[16,256]{1,0:T(8,128)S(1)} %add.20), channel_id=1, source_target_pairs={{0,4},{1,5},{2,6},{3,7},{4,0},{5,1},{6,2},{7,3},{8,12},{9,13},{10,... | collective-permute-start | bytes 49160 | tf_op jit(solution)/shard_map/ppermute | solution.py:436
  38.1 12.5 %collective-permute-start.3 = (f32[8,256]{1,0:T(8,128)S(1)}, f32[8,256]{1,0:T(8,128)S(1)}, u32[]{:S(2)}, u32[]{:S(2)}) collective-permute-start(f32[8,256]{1,0:T(8,128)S(1)} %get-tuple-element.17), channel_id=1, source_target_pairs={{0,64},{64,128},{128,192},{192,256},{256,320},{320,384},{384,448},... | collective-permute-start | bytes 24584 | tf_op jit(solution)/shard_map/ppermute | solution.py:438
  43.3 37.0 %copy-start = (bf16[128,256]{1,0:T(8,128)(2,1)S(1)}, bf16[128,256]{1,0:T(8,128)(2,1)}, u32[]{:S(2)}) copy-start(bf16[128,256]{1,0:T(8,128)(2,1)} %select.3.select_ref) | copy-start | bytes 196612
